TPU v7x, 256 devices: a whole 4x4x8 slice. The times are simulated.
256 devices in a mesh: box: 2 (over y_hi), gy: 16 (over y_lo, z), gz: 8 (over x, core).
Axes of the slice: x: 4, y: 4 (y_hi: 2, y_lo: 2; y = y_hi * 2 + y_lo), z: 8, core: 2. Of those that a mesh axis runs over, the one named last changes fastest.
Arguments:
- velocity: float32 [2, 3, 64, 256, 512], P('box', None, 'gz', 'gy'), may hold values from -6 to 6
- turbine_cells: int32 [8, 16, 512], P('gz', 'gy'), may hold values from 0 to 65535, as said below
- turbine_count: int32 [8, 16], P('gz', 'gy'), may hold values from 0 to 512, as said below
- fringe_start: int32 [1], replicated, may hold values from 0 to 384
Outputs:
- advanced: float32 [2, 3, 64, 256, 512], P('box', None, 'gz', 'gy')
Inputs may be any that keep to these rules, and one draw needn't show every extreme that they name: `turbine_cells`: flat indices into one device's block of 8 x 16 x 512 cells; cells may repeat. `turbine_count`: some device block has all 512 slots live; others have any number.
All inputs are finite; a program needn't handle non-finite values.
Results may differ from a plain program's by a relative error of at most 0.0003.
Values sent between devices are 32-bit elements; how exact they have to be, the bound alone decides.
A program may use at most 64 MiB of HBM per device.

v0:
```python
import jax
import jax.numpy as jnp
from jax import lax
from jax.sharding import PartitionSpec as P

FW = 128


smag_coef = 0.1024
drag_coef = 0.665
time_step = 0.2
tau_table = ((0, 3, 4), (3, 1, 5), (4, 5, 2))
pair_table = ((0, 0), (1, 1), (2, 2), (0, 1), (0, 2), (1, 2))


def extended(block, sides, width, periodic):
    for axis, dim in sides:
        count = lax.axis_size(axis)
        forward = [(i, i + 1) for i in range(count - 1)]
        if periodic:
            forward.append((count - 1, 0))
        backward = [(target, source) for source, target in forward]
        low = lax.ppermute(
            lax.slice_in_dim(block, block.shape[dim] - width, None, axis=dim), axis, forward
        )
        high = lax.ppermute(lax.slice_in_dim(block, 0, width, axis=dim), axis, backward)
        block = jnp.concatenate([low, block, high], axis=dim)
    return block


def shifted(value, axis, by):
    devices = lax.axis_size(axis)
    pairs = [(i, i + by) for i in range(devices) if 0 <= i + by < devices]
    return lax.ppermute(value, axis, pairs)


def xdiff(field):
    return (jnp.roll(field, -1, -1) - jnp.roll(field, 1, -1)) * 0.5


def sdiff(field, axis):
    count = field.shape[axis]
    return (
        lax.slice_in_dim(field, 2, count, axis=axis)
        - lax.slice_in_dim(field, 0, count - 2, axis=axis)
    ) * 0.5


def stress(grads):
    rates = [0.5 * (grads[j][i] + grads[i][j]) for i, j in pair_table]
    squares = rates[0] * rates[0] + rates[1] * rates[1] + rates[2] * rates[2]
    squares = squares + 2.0 * (rates[3] * rates[3] + rates[4] * rates[4] + rates[5] * rates[5])
    visc = smag_coef * jnp.sqrt(2.0 * squares)
    return jnp.stack([2.0 * visc * rate for rate in rates])


def divergence(tau_x, tau_y, tau_z):
    parts = []
    for i in range(3):
        term = xdiff(tau_x[tau_table[i][0]])
        term = term + sdiff(tau_y[tau_table[i][1]], 1)
        term = term + sdiff(tau_z[tau_table[i][2]], 0)
        parts.append(term)
    return jnp.stack(parts)


def advection(center, grads):
    return center[0] * grads[0] + center[1] * grads[1] + center[2] * grads[2]


def drag_force(ux, cells, count, is_main):
    flat = ux.reshape(-1)
    vals = flat[cells]
    live = jnp.arange(cells.shape[0]) < count
    force = jnp.where(live, -drag_coef * vals * jnp.abs(vals), 0.0)
    spread = jnp.zeros_like(flat).at[cells].add(force).reshape(ux.shape)
    return spread * is_main


def section_rates(field, cells, count, is_main):
    span_side = extended(field, (("gy", 2),), 1, True)
    vertical_side = extended(field, (("gz", 1),), 1, False)
    grads = [xdiff(field), sdiff(span_side, 2), sdiff(vertical_side, 1)]
    tau = stress(grads)
    tau_span = extended(tau, (("gy", 2),), 1, True)
    tau_vertical = extended(tau, (("gz", 1),), 1, False)
    div = divergence(tau, tau_span, tau_vertical)
    result = div - advection(field, grads)
    return result.at[0].add(drag_force(field[0], cells, count, is_main))


def blend(field, start, is_main):
    width = FW
    arrived = shifted(field, "box", 1)
    cols = jnp.arange(field.shape[3])
    inside = (cols >= start) & (cols < start + width) & (is_main > 0.5)
    return jnp.where(inside, 0.5 * (field + arrived), field)


def per_device(velocity, turbine_cells, turbine_count, fringe_start):
    field = velocity[0]
    cells = turbine_cells.reshape(-1)
    count = turbine_count.reshape(())
    start = fringe_start[0]
    is_main = (lax.axis_index("box") == 1).astype(jnp.float32)
    first = blend(field + time_step * section_rates(field, cells, count, is_main), start, is_main)
    second = blend(
        0.75 * field + 0.25 * (first + time_step * section_rates(first, cells, count, is_main)),
        start,
        is_main,
    )
    third = 1.0 / 3.0 * field + 2.0 / 3.0 * (
        second + time_step * section_rates(second, cells, count, is_main)
    )
    return blend(third, start, is_main)[None]


def solution(mesh):
    placed = (P("box", None, "gz", "gy", None), P("gz", "gy", None), P("gz", "gy"), P())
    return jax.shard_map(
        per_device,
        mesh=mesh,
        in_specs=placed,
        out_specs=P("box", None, "gz", "gy", None),
        check_vma=False,
    )
```

profile of v0, /device:TPU:17, one launch (start us, length us, event | category | flops | bytes accessed | tf_op | source)
XLA Modules:
  0.0 199.9 jit_solution(1134426070159885358)
XLA Ops:
  0.0 1.6 fusion.137
  1.6 2.6 %collective-permute-start.2 = (f32[3,1,16,512]{3,2,1,0:T(8,128)}, f32[3,1,16,512]{3,2,1,0:T(8,128)}, u32[]{:S(2)}, u32[]{:S(2)}) collective-permute-start(f32[3,1,16,512]{3,2,1,0:T(8,128)} %get-tuple-element.114), channel_id=1, source_target_pairs={{1,0},{2,1},{3,2},{4,3},{5,4},{6,5},{7,6},{9,8},{10,9},{11,10},{12... | collective-permute-start | bytes 294920 | tf_op jit(solution)/shard_map/ppermute | solution.py:26
  4.2 3.0 %collective-permute-start.3 = (f32[3,1,16,512]{3,2,1,0:T(8,128)}, f32[3,1,16,512]{3,2,1,0:T(8,128)}, u32[]{:S(2)}, u32[]{:S(2)}) collective-permute-start(f32[3,1,16,512]{3,2,1,0:T(8,128)} %get-tuple-element.115), channel_id=1, source_target_pairs={{0,1},{1,2},{2,3},{3,4},{4,5},{5,6},{6,7},{8,9},{9,10},{10,11},{11... | collective-permute-start | bytes 294920 | tf_op jit(solution)/shard_map/ppermute | solution.py:23
  7.2 1.8 fusion.138
  9.1 6.3 %collective-permute-start = (f32[3,8,1,512]{3,2,1,0:T(1,128)}, f32[3,8,1,512]{3,2,1,0:T(1,128)}, u32[]{:S(2)}, u32[]{:S(2)}) collective-permute-start(f32[3,8,1,512]{3,2,1,0:T(1,128)} %get-tuple-element.116), channel_id=1, source_target_pairs={{8,0},{16,8},{24,16},{32,24},{40,32},{48,40},{56,48},{64,56},{72,6... | collective-permute-start | bytes 147464 | tf_op jit(solution)/shard_map/ppermute | solution.py:26
  15.4 1.8 fusion.139
  17.3 0.9 fusion.136
  19.0 3.1 %gather_fusion = f32[512]{0:T(512)S(1)} fusion(f32[65536]{0:T(1024)S(1)} %bitcast.283, s32[1024]{0:T(1024)S(1)} %pad_clamp_fusion), kind=kCustom, calls=%fused_computation | custom fusion | bytes 6144 | tf_op jit(solution)/shard_map/gather | solution.py:73
  22.2 3.3 %scatter_custom_fusion = f32[65536]{0:T(1024)S(1)} fusion(s32[512]{0:T(512)S(1)} %bitcast.290, f32[512]{0:T(512)S(1)} %multiply_select_fusion.4, f32[]{:T(128)} %constant.99.clone.1), kind=kCustom, calls=%fused_computation.266 | custom fusion | flops 512 | bytes 262148 | tf_op jit(solution)/shard_map/scatter-add | solution.py:76
  25.5 0.7 broadcast_multiply_fusion.8
  26.6 1.7 mul.958
  28.3 1.2 broadcast_multiply_fusion.4
  31.1 3.6 %collective-permute-start.5 = (f32[6,8,1,512]{3,2,1,0:T(1,128)S(1)}, f32[6,8,1,512]{3,2,1,0:T(1,128)S(1)}, u32[]{:S(2)}, u32[]{:S(2)}) collective-permute-start(f32[6,8,1,512]{3,2,1,0:T(1,128)S(1)} %get-tuple-element.77), channel_id=1, source_target_pairs={{8,0},{16,8},{24,16},{32,24},{40,32},{48,40},{56,48},{64,56},{72,6... | collective-permute-start | bytes 294920 | tf_op jit(solution)/shard_map/ppermute | solution.py:26
  34.7 2.8 %collective-permute-start.6 = (f32[6,1,16,512]{3,2,1,0:T(8,128)S(1)}, f32[6,1,16,512]{3,2,1,0:T(8,128)S(1)}, u32[]{:S(2)}, u32[]{:S(2)}) collective-permute-start(f32[6,1,16,512]{3,2,1,0:T(8,128)S(1)} %get-tuple-element.78), channel_id=1, source_target_pairs={{1,0},{2,1},{3,2},{4,3},{5,4},{6,5},{7,6},{9,8},{10,9},{11,10},{12... | collective-permute-start | bytes 589832 | tf_op jit(solution)/shard_map/ppermute | solution.py:26
  37.4 2.8 %collective-permute-start.7 = (f32[6,1,16,512]{3,2,1,0:T(8,128)S(1)}, f32[6,1,16,512]{3,2,1,0:T(8,128)S(1)}, u32[]{:S(2)}, u32[]{:S(2)}) collective-permute-start(f32[6,1,16,512]{3,2,1,0:T(8,128)S(1)} %get-tuple-element.79), channel_id=1, source_target_pairs={{0,1},{1,2},{2,3},{3,4},{4,5},{5,6},{6,7},{8,9},{9,10},{10,11},{11... | collective-permute-start | bytes 589832 | tf_op jit(solution)/shard_map/ppermute | solution.py:23
  40.7 0.9 collective-permute-done.6
  41.6 1.2 collective-permute-done.7
  43.3 0.8 copy-done.14
  44.3 1.7 maximum_subtract_fusion.1
  46.2 1.3 collective-permute-start.8
  48.2 19.2 %collective-permute-done.8 = f32[3,8,16,512]{3,2,1,0:T(8,128)S(1)} collective-permute-done((f32[3,8,16,512]{3,2,1,0:T(8,128)S(1)}, f32[3,8,16,512]{3,2,1,0:T(8,128)S(1)}, u32[]{:S(2)}, u32[]{:S(2)}) %collective-permute-start.8) | collective-permute-done | bytes 786464 | tf_op jit(solution)/shard_map/ppermute | solution.py:34
  68.4 0.7 fusion.133
  69.4 0.8 fusion.135
  70.2 0.9 fusion.131
  71.1 1.9 collective-permute-start.11
  73.0 5.2 %collective-permute-start.12 = (f32[3,1,16,512]{3,2,1,0:T(8,128)}, f32[3,1,16,512]{3,2,1,0:T(8,128)}, u32[]{:S(2)}, u32[]{:S(2)}) collective-permute-start(f32[3,1,16,512]{3,2,1,0:T(8,128)} %get-tuple-element.101), channel_id=1, source_target_pairs={{0,1},{1,2},{2,3},{3,4},{4,5},{5,6},{6,7},{8,9},{9,10},{10,11},{11... | collective-permute-start | bytes 294920 | tf_op jit(solution)/shard_map/ppermute | solution.py:23
  78.3 3.6 %collective-permute-start.9 = (f32[3,8,1,512]{3,2,1,0:T(1,128)}, f32[3,8,1,512]{3,2,1,0:T(1,128)}, u32[]{:S(2)}, u32[]{:S(2)}) collective-permute-start(f32[3,8,1,512]{3,2,1,0:T(1,128)} %get-tuple-element.102), channel_id=1, source_target_pairs={{8,0},{16,8},{24,16},{32,24},{40,32},{48,40},{56,48},{64,56},{72,6... | collective-permute-start | bytes 147464 | tf_op jit(solution)/shard_map/ppermute | solution.py:26
  81.9 4.4 %gather_fusion.1 = f32[512]{0:T(512)} fusion(f32[65536]{0:T(1024)S(1)} %bitcast.285, s32[1024]{0:T(1024)} %copy-done.17), kind=kCustom, calls=%fused_computation.1 | custom fusion | bytes 6144 | tf_op jit(solution)/shard_map/gather | solution.py:73
  86.3 1.3 multiply_select_fusion.3
  87.6 3.5 %scatter_custom_fusion.1 = f32[65536]{0:T(1024)S(1)} fusion(s32[512]{0:T(512)} %bitcast.291, f32[512]{0:T(512)} %multiply_select_fusion.3, f32[]{:T(128)} %constant.99.clone.1), kind=kCustom, calls=%fused_computation.264 | custom fusion | flops 512 | bytes 262656 | tf_op jit(solution)/shard_map/scatter-add | solution.py:76
  91.1 0.7 broadcast_multiply_fusion.7
  91.8 2.2 %broadcast_multiply_fusion.3 = f32[3,8,16,512]{3,2,1,0:T(8,128)} fusion(f32[3,8,16,511]{3,2,1,0:T(8,128)S(1)} %get-tuple-element.105, f32[3,8,16,1]{3,2,1,0:T(8,128)} %get-tuple-element.107, f32[3,8,16,1]{3,2,1,0:T(8,128)} %get-tuple-element.106, f32[3,8,16,511]{3,2,1,0:T(8,128)S(1)} %get-tuple-element.104), kind=kLoop, calls=%fused_computation.57 | loop fusion | flops 786432 | bytes 2359296 | tf_op jit(solution)/shard_map/mul | solution.py:38
  94.0 1.0 mul.1018
  95.1 1.2 broadcast_multiply_fusion.2
  98.0 3.6 %collective-permute-start.14 = (f32[6,8,1,512]{3,2,1,0:T(1,128)S(1)}, f32[6,8,1,512]{3,2,1,0:T(1,128)S(1)}, u32[]{:S(2)}, u32[]{:S(2)}) collective-permute-start(f32[6,8,1,512]{3,2,1,0:T(1,128)S(1)} %get-tuple-element.73), channel_id=1, source_target_pairs={{8,0},{16,8},{24,16},{32,24},{40,32},{48,40},{56,48},{64,56},{72,6... | collective-permute-start | bytes 294920 | tf_op jit(solution)/shard_map/ppermute | solution.py:26
  101.5 1.9 collective-permute-start.15
  103.5 3.6 %collective-permute-start.16 = (f32[6,1,16,512]{3,2,1,0:T(8,128)S(1)}, f32[6,1,16,512]{3,2,1,0:T(8,128)S(1)}, u32[]{:S(2)}, u32[]{:S(2)}) collective-permute-start(f32[6,1,16,512]{3,2,1,0:T(8,128)S(1)} %get-tuple-element.75), channel_id=1, source_target_pairs={{0,1},{1,2},{2,3},{3,4},{4,5},{5,6},{6,7},{8,9},{9,10},{10,11},{11... | collective-permute-start | bytes 589832 | tf_op jit(solution)/shard_map/ppermute | solution.py:23
  107.6 0.9 collective-permute-done.15
  108.5 1.2 collective-permute-done.16
  111.4 1.6 maximum_subtract_fusion.3
  113.3 1.3 collective-permute-start.17
  114.6 19.1 %collective-permute-done.17 = f32[3,8,16,512]{3,2,1,0:T(8,128)S(1)} collective-permute-done((f32[3,8,16,512]{3,2,1,0:T(8,128)S(1)}, f32[3,8,16,512]{3,2,1,0:T(8,128)S(1)}, u32[]{:S(2)}, u32[]{:S(2)}) %collective-permute-start.17) | collective-permute-done | bytes 786464 | tf_op jit(solution)/shard_map/ppermute | solution.py:34
  134.6 0.7 fusion.128
  135.6 0.8 fusion.130
  136.4 0.9 fusion.126
  137.3 1.9 collective-permute-start.20
  139.2 6.0 %collective-permute-start.21 = (f32[3,1,16,512]{3,2,1,0:T(8,128)}, f32[3,1,16,512]{3,2,1,0:T(8,128)}, u32[]{:S(2)}, u32[]{:S(2)}) collective-permute-start(f32[3,1,16,512]{3,2,1,0:T(8,128)} %get-tuple-element.87), channel_id=1, source_target_pairs={{0,1},{1,2},{2,3},{3,4},{4,5},{5,6},{6,7},{8,9},{9,10},{10,11},{11... | collective-permute-start | bytes 294920 | tf_op jit(solution)/shard_map/ppermute | solution.py:23
  145.3 1.5 collective-permute-start.19
  146.8 4.4 %gather_fusion.2 = f32[512]{0:T(512)} fusion(f32[65536]{0:T(1024)S(1)} %bitcast.284, s32[1024]{0:T(1024)} %copy-done.17), kind=kCustom, calls=%fused_computation.2 | custom fusion | bytes 6144 | tf_op jit(solution)/shard_map/gather | solution.py:73
  151.2 1.3 multiply_select_fusion.2
  152.5 3.7 %scatter_custom_fusion.2 = f32[65536]{0:T(1024)S(1)} fusion(s32[512]{0:T(512)} %bitcast.292, f32[512]{0:T(512)} %multiply_select_fusion.2, f32[]{:T(128)} %constant.99.clone.1), kind=kCustom, calls=%fused_computation.262 | custom fusion | flops 512 | bytes 262656 | tf_op jit(solution)/shard_map/scatter-add | solution.py:76
  156.2 0.7 broadcast_multiply_fusion.6
  156.9 2.2 %broadcast_multiply_fusion.1 = f32[3,8,16,512]{3,2,1,0:T(8,128)} fusion(f32[3,8,16,511]{3,2,1,0:T(8,128)S(1)} %get-tuple-element.91, f32[3,8,16,1]{3,2,1,0:T(8,128)} %get-tuple-element.93, f32[3,8,16,1]{3,2,1,0:T(8,128)} %get-tuple-element.92, f32[3,8,16,511]{3,2,1,0:T(8,128)S(1)} %get-tuple-element.90), kind=kLoop, calls=%fused_computation.55 | loop fusion | flops 786432 | bytes 2359296 | tf_op jit(solution)/shard_map/mul | solution.py:38
  159.1 1.0 mul.1080
  160.2 1.2 broadcast_multiply_fusion
  163.1 3.6 %collective-permute-start.23 = (f32[6,8,1,512]{3,2,1,0:T(1,128)S(1)}, f32[6,8,1,512]{3,2,1,0:T(1,128)S(1)}, u32[]{:S(2)}, u32[]{:S(2)}) collective-permute-start(f32[6,8,1,512]{3,2,1,0:T(1,128)S(1)} %get-tuple-element.69), channel_id=1, source_target_pairs={{8,0},{16,8},{24,16},{32,24},{40,32},{48,40},{56,48},{64,56},{72,6... | collective-permute-start | bytes 294920 | tf_op jit(solution)/shard_map/ppermute | solution.py:26
  166.7 1.9 collective-permute-start.24
  168.6 3.6 %collective-permute-start.25 = (f32[6,1,16,512]{3,2,1,0:T(8,128)S(1)}, f32[6,1,16,512]{3,2,1,0:T(8,128)S(1)}, u32[]{:S(2)}, u32[]{:S(2)}) collective-permute-start(f32[6,1,16,512]{3,2,1,0:T(8,128)S(1)} %get-tuple-element.71), channel_id=1, source_target_pairs={{0,1},{1,2},{2,3},{3,4},{4,5},{5,6},{6,7},{8,9},{9,10},{10,11},{11... | collective-permute-start | bytes 589832 | tf_op jit(solution)/shard_map/ppermute | solution.py:23
  172.7 0.9 collective-permute-done.24
  173.7 1.2 collective-permute-done.25
  176.5 1.6 maximum_subtract_fusion.5
  178.5 1.3 collective-permute-start.26
  179.8 19.1 %collective-permute-done.26 = f32[3,8,16,512]{3,2,1,0:T(8,128)S(1)} collective-permute-done((f32[3,8,16,512]{3,2,1,0:T(8,128)S(1)}, f32[3,8,16,512]{3,2,1,0:T(8,128)S(1)}, u32[]{:S(2)}, u32[]{:S(2)}) %collective-permute-start.26) | collective-permute-done | bytes 786464 | tf_op jit(solution)/shard_map/ppermute | solution.py:34
  198.8 1.0 select_bitcast_fusion
  (148 shorter events, 13.9 us)
Async XLA Ops:
  1.6 26.6 %collective-permute-start.2 = (f32[3,1,16,512]{3,2,1,0:T(8,128)}, f32[3,1,16,512]{3,2,1,0:T(8,128)}, u32[]{:S(2)}, u32[]{:S(2)}) collective-permute-start(f32[3,1,16,512]{3,2,1,0:T(8,128)} %get-tuple-element.114), channel_id=1, source_target_pairs={{1,0},{2,1},{3,2},{4,3},{5,4},{6,5},{7,6},{9,8},{10,9},{11,10},{12... | collective-permute-start | bytes 294920 | tf_op jit(solution)/shard_map/ppermute | solution.py:26
  4.2 24.1 %collective-permute-start.3 = (f32[3,1,16,512]{3,2,1,0:T(8,128)}, f32[3,1,16,512]{3,2,1,0:T(8,128)}, u32[]{:S(2)}, u32[]{:S(2)}) collective-permute-start(f32[3,1,16,512]{3,2,1,0:T(8,128)} %get-tuple-element.115), channel_id=1, source_target_pairs={{0,1},{1,2},{2,3},{3,4},{4,5},{5,6},{6,7},{8,9},{9,10},{10,11},{11... | collective-permute-start | bytes 294920 | tf_op jit(solution)/shard_map/ppermute | solution.py:23
  9.1 19.2 %collective-permute-start = (f32[3,8,1,512]{3,2,1,0:T(1,128)}, f32[3,8,1,512]{3,2,1,0:T(1,128)}, u32[]{:S(2)}, u32[]{:S(2)}) collective-permute-start(f32[3,8,1,512]{3,2,1,0:T(1,128)} %get-tuple-element.116), channel_id=1, source_target_pairs={{8,0},{16,8},{24,16},{32,24},{40,32},{48,40},{56,48},{64,56},{72,6... | collective-permute-start | bytes 147464 | tf_op jit(solution)/shard_map/ppermute | solution.py:26
  15.4 1.8 copy-start
  15.4 12.9 %collective-permute-start.1 = (f32[3,8,1,512]{3,2,1,0:T(1,128)}, f32[3,8,1,512]{3,2,1,0:T(1,128)}, u32[]{:S(2)}, u32[]{:S(2)}) collective-permute-start(f32[3,8,1,512]{3,2,1,0:T(1,128)} %get-tuple-element.117), channel_id=1, source_target_pairs={{0,8},{8,16},{16,24},{24,32},{32,40},{40,48},{48,56},{56,64},{64,7... | collective-permute-start | bytes 147464 | tf_op jit(solution)/shard_map/ppermute | solution.py:23
  17.2 1.0 copy-start.22
  18.2 8.0 %copy-start.21 = (s32[512,1]{0,1:T(1,128)}, s32[512,1]{0,1:T(1,128)S(1)}, u32[]{:S(2)}) copy-start(s32[512,1]{0,1:T(1,128)S(1)} %compare_select_fusion) | copy-start | bytes 6148
  18.3 8.0 %copy-start.17 = (s32[1024]{0:T(1024)}, s32[1024]{0:T(1024)S(1)}, u32[]{:S(2)}) copy-start(s32[1024]{0:T(1024)S(1)} %pad_clamp_fusion) | copy-start | bytes 12292
  31.0 9.4 %collective-permute-start.4 = (f32[6,8,1,512]{3,2,1,0:T(1,128)S(1)}, f32[6,8,1,512]{3,2,1,0:T(1,128)S(1)}, u32[]{:S(2)}, u32[]{:S(2)}) collective-permute-start(f32[6,8,1,512]{3,2,1,0:T(1,128)S(1)} %get-tuple-element.76), channel_id=1, source_target_pairs={{0,8},{8,16},{16,24},{24,32},{32,40},{40,48},{48,56},{56,64},{64,7... | collective-permute-start | bytes 294920 | tf_op jit(solution)/shard_map/ppermute | solution.py:23
  31.1 9.4 %collective-permute-start.5 = (f32[6,8,1,512]{3,2,1,0:T(1,128)S(1)}, f32[6,8,1,512]{3,2,1,0:T(1,128)S(1)}, u32[]{:S(2)}, u32[]{:S(2)}) collective-permute-start(f32[6,8,1,512]{3,2,1,0:T(1,128)S(1)} %get-tuple-element.77), channel_id=1, source_target_pairs={{8,0},{16,8},{24,16},{32,24},{40,32},{48,40},{56,48},{64,56},{72,6... | collective-permute-start | bytes 294920 | tf_op jit(solution)/shard_map/ppermute | solution.py:26
  34.7 7.0 %collective-permute-start.6 = (f32[6,1,16,512]{3,2,1,0:T(8,128)S(1)}, f32[6,1,16,512]{3,2,1,0:T(8,128)S(1)}, u32[]{:S(2)}, u32[]{:S(2)}) collective-permute-start(f32[6,1,16,512]{3,2,1,0:T(8,128)S(1)} %get-tuple-element.78), channel_id=1, source_target_pairs={{1,0},{2,1},{3,2},{4,3},{5,4},{6,5},{7,6},{9,8},{10,9},{11,10},{12... | collective-permute-start | bytes 589832 | tf_op jit(solution)/shard_map/ppermute | solution.py:26
  37.4 5.4 %collective-permute-start.7 = (f32[6,1,16,512]{3,2,1,0:T(8,128)S(1)}, f32[6,1,16,512]{3,2,1,0:T(8,128)S(1)}, u32[]{:S(2)}, u32[]{:S(2)}) collective-permute-start(f32[6,1,16,512]{3,2,1,0:T(8,128)S(1)} %get-tuple-element.79), channel_id=1, source_target_pairs={{0,1},{1,2},{2,3},{3,4},{4,5},{5,6},{6,7},{8,9},{9,10},{10,11},{11... | collective-permute-start | bytes 589832 | tf_op jit(solution)/shard_map/ppermute | solution.py:23
  43.1 1.0 copy-start.14
  43.2 1.0 copy-start.15
  43.2 1.1 copy-start.16
  44.3 1.7 copy-start.7
  46.2 21.2 %collective-permute-start.8 = (f32[3,8,16,512]{3,2,1,0:T(8,128)S(1)}, f32[3,8,16,512]{3,2,1,0:T(8,128)S(1)}, u32[]{:S(2)}, u32[]{:S(2)}) collective-permute-start(f32[3,8,16,512]{3,2,1,0:T(8,128)S(1)} %multiply_add_fusion.2), channel_id=1, source_target_pairs={{0,128},{1,129},{2,130},{3,131},{4,132},{5,133},{6,134},{7,135},{8... | collective-permute-start | bytes 2359304 | tf_op jit(solution)/shard_map/ppermute | solution.py:34
  48.2 20.2 %copy-start.18 = (pred[512]{0:T(512)(128)(4,1)}, pred[512]{0:T(512)(128)(4,1)S(1)}, u32[]{:S(2)}) copy-start(pred[512]{0:T(512)(128)(4,1)S(1)} %fusion.110) | copy-start | bytes 1540
  71.1 23.9 %collective-permute-start.11 = (f32[3,1,16,512]{3,2,1,0:T(8,128)}, f32[3,1,16,512]{3,2,1,0:T(8,128)S(1)}, u32[]{:S(2)}, u32[]{:S(2)}) collective-permute-start(f32[3,1,16,512]{3,2,1,0:T(8,128)} %get-tuple-element.100), channel_id=1, source_target_pairs={{1,0},{2,1},{3,2},{4,3},{5,4},{6,5},{7,6},{9,8},{10,9},{11,10},{12... | collective-permute-start | bytes 294920 | tf_op jit(solution)/shard_map/ppermute | solution.py:26
  73.0 22.0 %collective-permute-start.12 = (f32[3,1,16,512]{3,2,1,0:T(8,128)}, f32[3,1,16,512]{3,2,1,0:T(8,128)}, u32[]{:S(2)}, u32[]{:S(2)}) collective-permute-start(f32[3,1,16,512]{3,2,1,0:T(8,128)} %get-tuple-element.101), channel_id=1, source_target_pairs={{0,1},{1,2},{2,3},{3,4},{4,5},{5,6},{6,7},{8,9},{9,10},{10,11},{11... | collective-permute-start | bytes 294920 | tf_op jit(solution)/shard_map/ppermute | solution.py:23
  78.2 16.8 %collective-permute-start.10 = (f32[3,8,1,512]{3,2,1,0:T(1,128)}, f32[3,8,1,512]{3,2,1,0:T(1,128)S(1)}, u32[]{:S(2)}, u32[]{:S(2)}) collective-permute-start(f32[3,8,1,512]{3,2,1,0:T(1,128)} %get-tuple-element.103), channel_id=1, source_target_pairs={{0,8},{8,16},{16,24},{24,32},{32,40},{40,48},{48,56},{56,64},{64,7... | collective-permute-start | bytes 147464 | tf_op jit(solution)/shard_map/ppermute | solution.py:23
  78.3 16.8 %collective-permute-start.9 = (f32[3,8,1,512]{3,2,1,0:T(1,128)}, f32[3,8,1,512]{3,2,1,0:T(1,128)}, u32[]{:S(2)}, u32[]{:S(2)}) collective-permute-start(f32[3,8,1,512]{3,2,1,0:T(1,128)} %get-tuple-element.102), channel_id=1, source_target_pairs={{8,0},{16,8},{24,16},{32,24},{40,32},{48,40},{56,48},{64,56},{72,6... | collective-permute-start | bytes 147464 | tf_op jit(solution)/shard_map/ppermute | solution.py:26
  95.0 1.3 copy-start.1
  97.9 9.4 %collective-permute-start.13 = (f32[6,8,1,512]{3,2,1,0:T(1,128)S(1)}, f32[6,8,1,512]{3,2,1,0:T(1,128)S(1)}, u32[]{:S(2)}, u32[]{:S(2)}) collective-permute-start(f32[6,8,1,512]{3,2,1,0:T(1,128)S(1)} %get-tuple-element.72), channel_id=1, source_target_pairs={{0,8},{8,16},{16,24},{24,32},{32,40},{40,48},{48,56},{56,64},{64,7... | collective-permute-start | bytes 294920 | tf_op jit(solution)/shard_map/ppermute | solution.py:23
  98.0 9.4 %collective-permute-start.14 = (f32[6,8,1,512]{3,2,1,0:T(1,128)S(1)}, f32[6,8,1,512]{3,2,1,0:T(1,128)S(1)}, u32[]{:S(2)}, u32[]{:S(2)}) collective-permute-start(f32[6,8,1,512]{3,2,1,0:T(1,128)S(1)} %get-tuple-element.73), channel_id=1, source_target_pairs={{8,0},{16,8},{24,16},{32,24},{40,32},{48,40},{56,48},{64,56},{72,6... | collective-permute-start | bytes 294920 | tf_op jit(solution)/shard_map/ppermute | solution.py:26
  101.5 7.0 %collective-permute-start.15 = (f32[6,1,16,512]{3,2,1,0:T(8,128)S(1)}, f32[6,1,16,512]{3,2,1,0:T(8,128)S(1)}, u32[]{:S(2)}, u32[]{:S(2)}) collective-permute-start(f32[6,1,16,512]{3,2,1,0:T(8,128)S(1)} %get-tuple-element.74), channel_id=1, source_target_pairs={{1,0},{2,1},{3,2},{4,3},{5,4},{6,5},{7,6},{9,8},{10,9},{11,10},{12... | collective-permute-start | bytes 589832 | tf_op jit(solution)/shard_map/ppermute | solution.py:26
  103.5 6.2 %collective-permute-start.16 = (f32[6,1,16,512]{3,2,1,0:T(8,128)S(1)}, f32[6,1,16,512]{3,2,1,0:T(8,128)S(1)}, u32[]{:S(2)}, u32[]{:S(2)}) collective-permute-start(f32[6,1,16,512]{3,2,1,0:T(8,128)S(1)} %get-tuple-element.75), channel_id=1, source_target_pairs={{0,1},{1,2},{2,3},{3,4},{4,5},{5,6},{6,7},{8,9},{9,10},{10,11},{11... | collective-permute-start | bytes 589832 | tf_op jit(solution)/shard_map/ppermute | solution.py:23
  110.0 0.9 copy-start.5
  110.0 1.0 copy-start.6
  110.1 1.1 copy-start.11
  110.1 1.2 copy-start.12
  110.1 1.3 copy-start.13
  113.1 20.6 %copy-start.19 = (pred[512]{0:T(512)(128)(4,1)S(1)}, pred[512]{0:T(512)(128)(4,1)}, u32[]{:S(2)}) copy-start(pred[512]{0:T(512)(128)(4,1)} %copy-done.18) | copy-start | bytes 1540
  113.3 20.4 %collective-permute-start.17 = (f32[3,8,16,512]{3,2,1,0:T(8,128)S(1)}, f32[3,8,16,512]{3,2,1,0:T(8,128)S(1)}, u32[]{:S(2)}, u32[]{:S(2)}) collective-permute-start(f32[3,8,16,512]{3,2,1,0:T(8,128)S(1)} %multiply_add_fusion.1), channel_id=1, source_target_pairs={{0,128},{1,129},{2,130},{3,131},{4,132},{5,133},{6,134},{7,135},{8... | collective-permute-start | bytes 2359304 | tf_op jit(solution)/shard_map/ppermute | solution.py:34
  137.3 22.9 %collective-permute-start.20 = (f32[3,1,16,512]{3,2,1,0:T(8,128)}, f32[3,1,16,512]{3,2,1,0:T(8,128)S(1)}, u32[]{:S(2)}, u32[]{:S(2)}) collective-permute-start(f32[3,1,16,512]{3,2,1,0:T(8,128)} %get-tuple-element.86), channel_id=1, source_target_pairs={{1,0},{2,1},{3,2},{4,3},{5,4},{6,5},{7,6},{9,8},{10,9},{11,10},{12... | collective-permute-start | bytes 294920 | tf_op jit(solution)/shard_map/ppermute | solution.py:26
  139.2 20.9 %collective-permute-start.21 = (f32[3,1,16,512]{3,2,1,0:T(8,128)}, f32[3,1,16,512]{3,2,1,0:T(8,128)}, u32[]{:S(2)}, u32[]{:S(2)}) collective-permute-start(f32[3,1,16,512]{3,2,1,0:T(8,128)} %get-tuple-element.87), channel_id=1, source_target_pairs={{0,1},{1,2},{2,3},{3,4},{4,5},{5,6},{6,7},{8,9},{9,10},{10,11},{11... | collective-permute-start | bytes 294920 | tf_op jit(solution)/shard_map/ppermute | solution.py:23
  145.2 14.9 %collective-permute-start.18 = (f32[3,8,1,512]{3,2,1,0:T(1,128)}, f32[3,8,1,512]{3,2,1,0:T(1,128)S(1)}, u32[]{:S(2)}, u32[]{:S(2)}) collective-permute-start(f32[3,8,1,512]{3,2,1,0:T(1,128)} %get-tuple-element.88), channel_id=1, source_target_pairs={{8,0},{16,8},{24,16},{32,24},{40,32},{48,40},{56,48},{64,56},{72,6... | collective-permute-start | bytes 147464 | tf_op jit(solution)/shard_map/ppermute | solution.py:26
  145.3 14.9 %collective-permute-start.19 = (f32[3,8,1,512]{3,2,1,0:T(1,128)}, f32[3,8,1,512]{3,2,1,0:T(1,128)}, u32[]{:S(2)}, u32[]{:S(2)}) collective-permute-start(f32[3,8,1,512]{3,2,1,0:T(1,128)} %get-tuple-element.89), channel_id=1, source_target_pairs={{0,8},{8,16},{16,24},{24,32},{32,40},{40,48},{48,56},{56,64},{64,7... | collective-permute-start | bytes 147464 | tf_op jit(solution)/shard_map/ppermute | solution.py:23
  160.1 1.3 copy-start.2
  163.0 9.4 %collective-permute-start.22 = (f32[6,8,1,512]{3,2,1,0:T(1,128)S(1)}, f32[6,8,1,512]{3,2,1,0:T(1,128)S(1)}, u32[]{:S(2)}, u32[]{:S(2)}) collective-permute-start(f32[6,8,1,512]{3,2,1,0:T(1,128)S(1)} %get-tuple-element.68), channel_id=1, source_target_pairs={{0,8},{8,16},{16,24},{24,32},{32,40},{40,48},{48,56},{56,64},{64,7... | collective-permute-start | bytes 294920 | tf_op jit(solution)/shard_map/ppermute | solution.py:23
  163.1 9.4 %collective-permute-start.23 = (f32[6,8,1,512]{3,2,1,0:T(1,128)S(1)}, f32[6,8,1,512]{3,2,1,0:T(1,128)S(1)}, u32[]{:S(2)}, u32[]{:S(2)}) collective-permute-start(f32[6,8,1,512]{3,2,1,0:T(1,128)S(1)} %get-tuple-element.69), channel_id=1, source_target_pairs={{8,0},{16,8},{24,16},{32,24},{40,32},{48,40},{56,48},{64,56},{72,6... | collective-permute-start | bytes 294920 | tf_op jit(solution)/shard_map/ppermute | solution.py:26
  166.7 7.0 %collective-permute-start.24 = (f32[6,1,16,512]{3,2,1,0:T(8,128)S(1)}, f32[6,1,16,512]{3,2,1,0:T(8,128)S(1)}, u32[]{:S(2)}, u32[]{:S(2)}) collective-permute-start(f32[6,1,16,512]{3,2,1,0:T(8,128)S(1)} %get-tuple-element.70), channel_id=1, source_target_pairs={{1,0},{2,1},{3,2},{4,3},{5,4},{6,5},{7,6},{9,8},{10,9},{11,10},{12... | collective-permute-start | bytes 589832 | tf_op jit(solution)/shard_map/ppermute | solution.py:26
  168.6 6.2 %collective-permute-start.25 = (f32[6,1,16,512]{3,2,1,0:T(8,128)S(1)}, f32[6,1,16,512]{3,2,1,0:T(8,128)S(1)}, u32[]{:S(2)}, u32[]{:S(2)}) collective-permute-start(f32[6,1,16,512]{3,2,1,0:T(8,128)S(1)} %get-tuple-element.71), channel_id=1, source_target_pairs={{0,1},{1,2},{2,3},{3,4},{4,5},{5,6},{6,7},{8,9},{9,10},{10,11},{11... | collective-permute-start | bytes 589832 | tf_op jit(solution)/shard_map/ppermute | solution.py:23
  175.2 0.9 copy-start.3
  175.2 1.0 copy-start.4
  175.2 1.1 copy-start.8
  175.2 1.2 copy-start.9
  175.2 1.3 copy-start.10
  178.2 20.7 %copy-start.20 = (pred[512]{0:T(512)(128)(4,1)S(1)}, pred[512]{0:T(512)(128)(4,1)}, u32[]{:S(2)}) copy-start(pred[512]{0:T(512)(128)(4,1)} %copy-done.18) | copy-start | bytes 1540
  178.5 20.4 %collective-permute-start.26 = (f32[3,8,16,512]{3,2,1,0:T(8,128)S(1)}, f32[3,8,16,512]{3,2,1,0:T(8,128)S(1)}, u32[]{:S(2)}, u32[]{:S(2)}) collective-permute-start(f32[3,8,16,512]{3,2,1,0:T(8,128)S(1)} %multiply_add_fusion), channel_id=1, source_target_pairs={{0,128},{1,129},{2,130},{3,131},{4,132},{5,133},{6,134},{7,135},{8... | collective-permute-start | bytes 2359304 | tf_op jit(solution)/shard_map/ppermute | solution.py:34
where the time goes:
time: 202 us; the launch traced here: 200 us
  waiting for transfers between devices  63.8 us (32%)
  starting transfers between devices  63.4 us (31%)
  other arithmetic  38.4 us (19%)
  local copies, waits for them, and re-layouts  31.9 us (16%)
  between operations  2.34 us (1%)
    ppermute x3, waiting for transfers between devices, shifted(): return lax.ppermute(value, axis, pairs)  57.3 us
    ppermute x12, starting transfers between devices, extended(): lax.ppermute(lax.slice_in_dim(block, 0, width, axis=dim), axis, backward)  33.6 us
    ppermute x12, starting transfers between devices, extended(): lax.ppermute(lax.slice_in_dim(block, block.shape[dim] - width, None, axis...  26 us
    gather x3, local copies, waits for them, and re-layouts, drag_force(): vals = flat[cells]  12 us
    scatter-add x3, other arithmetic, drag_force(): spread = jnp.zeros_like(flat).at[cells].add(force).reshape(ux.shape)  10.5 us
    slice x9, local copies, waits for them, and re-layouts, extended(): lax.slice_in_dim(block, 0, width, axis=dim)  6.38 us
    slice x22, local copies, waits for them, and re-layouts, xdiff(): return (jnp.roll(field, -1, -1) - jnp.roll(field, 1, -1)) * 0.5  5.94 us
    sub x3, other arithmetic, section_rates(): result = div - advection(field, grads)  4.96 us
  transfers between devices with their start and end apart: 27, of which 9 were waited for; matrix products, arithmetic and copies ran while one was open for 21% of the time, Pallas kernels for 0%

commit v1 on v0

v1 whole, which is shorter than its diff:
```python
import functools

import jax
import jax.numpy as jnp
from jax import lax
from jax.experimental import pallas as pl
from jax.experimental.pallas import tpu as pltpu
from jax.sharding import PartitionSpec as P

MESH = pl.DeviceIdType.MESH
CZ, CY, NX = 8, 16, 512
LANES = 128
LT = NX // LANES
PY = 32
ZU = CZ + 4
ZT = CZ + 2
SPAN = LT * PY

smag_coef = 0.1024
drag_coef = 0.665
time_step = 0.2
TINY = 1e-37
XX, YY, ZZ, XY, XZ, YZ = range(6)
STAGES = ((0.0, 1.0), (0.75, 0.25), (1.0 / 3.0, 2.0 / 3.0))
CORNERS = ((-1, -1), (-1, 1), (1, -1), (1, 1))
Z_DOWN, Z_UP, Y_DOWN, Y_UP, CORNER, BOX = 0, 1, 2, 3, 4, 8
COPIES = 9


def kernel(
    nz, ny, start, count, cells, vel, out, u, tau, acc, raw, cnt, sy, ry, cs, cr, arrived, io_sem, send_sem, recv_sem
):
    gz, gy, box = lax.axis_index("gz"), lax.axis_index("gy"), lax.axis_index("box")
    up, down = lax.rem(gy + 1, ny), lax.rem(gy + ny - 1, ny)
    has_below, has_above = gz > 0, gz < nz - 1
    is_main = box == 1
    has = {-1: has_below, 1: has_above}
    beside = {-1: down, 1: up}

    loads = [
        pltpu.make_async_copy(
            vel.at[0, :, :, :, pl.ds(l * LANES, LANES)], raw.at[:, :, l], io_sem.at[l]
        )
        for l in range(LT)
    ]
    for copy in loads:
        copy.start()

    barrier = pltpu.get_barrier_semaphore()

    def greet(where):
        pl.semaphore_signal(barrier, inc=1, device_id=where, device_id_type=MESH)

    greet({"gy": down})
    greet({"gy": up})
    greet({"box": 1 - box})
    for a in (-1, 1):

        @pl.when(has[a])
        def _(a=a):
            greet({"gz": gz + a})
            greet({"gz": gz + a, "gy": down})
            greet({"gz": gz + a, "gy": up})

    lane = lax.broadcasted_iota(jnp.int32, (8, LANES), 1)
    first_lane, last_lane = lane == 0, lane == LANES - 1

    flat = [u.at[k].reshape(3 * ZU * SPAN, LANES) for k in range(4)]
    layers = [u.at[k].reshape(3 * ZU, SPAN, LANES) for k in range(4)]
    tau_flat = tau.reshape(6 * ZT * SPAN, LANES)
    tau_layers = tau.reshape(6 * ZT, SPAN, LANES)

    zeros = jnp.zeros((8, LANES), jnp.float32)
    for a, at in ((-1, 0), (1, CZ + 2)):

        @pl.when(jnp.logical_not(has[a]))
        def _(a=a, at=at):
            def clear(k):
                for c in range(3):
                    for z in range(2):
                        for l in range(LT):
                            for r in range(0, PY, 8):
                                u[k, c, at + z, l, pl.ds(r, 8), :] = zeros
                for side in range(2):
                    for c in range(3):
                        for l in range(LT):
                            ry[k, side, 0, c, l, pl.ds(0 if a < 0 else 16, 8), :] = zeros

            for k in range(3):
                clear(k)

    s = start[0]
    flat_cells = cells[...]
    row = lax.shift_right_logical(flat_cells, 9)
    col = (flat_cells - s) & (NX - 1)
    slots = cells.shape[1]
    live = lax.broadcasted_iota(jnp.int32, (1, slots), 1) < count[0, 0]
    row = jnp.where(live, row, -1)
    rows = lax.broadcasted_iota(jnp.int32, (CZ * CY, slots), 0)
    cols = lax.broadcasted_iota(jnp.int32, (NX, slots), 0)
    pick_row = jnp.where(rows == row, 1.0, 0.0).astype(jnp.bfloat16)
    pick_col = jnp.where(cols == col, 1.0, 0.0).astype(jnp.bfloat16)
    times = lax.dot_general(
        pick_row, pick_col, (((1,), (1,)), ((), ())), preferred_element_type=jnp.float32
    )
    times = times * jnp.where(is_main, -drag_coef * time_step, 0.0)
    for l in range(LT):
        cnt[:, l] = times[:, l * LANES : (l + 1) * LANES].reshape(CZ, CY, LANES)

    q = lax.shift_right_logical(s, 7)
    r = s & (LANES - 1)
    left = (LANES - r) & (LANES - 1)
    keep = lane < LANES - r
    for copy in loads:
        copy.wait()

    def rotate_in(z, carry):
        for c in range(3):
            for h in range(0, CY, 8):
                tiles = [
                    pltpu.roll(raw[c, z, (l + q) & (LT - 1), pl.ds(h, 8), :], left, 1)
                    for l in range(LT)
                ]
                for l in range(LT):
                    u[0, c, z + 2, l, pl.ds(8 + h, 8), :] = jnp.where(
                        keep, tiles[l], tiles[(l + 1) % LT]
                    )
        return carry

    lax.fori_loop(0, CZ, rotate_in, 0)

    pl.semaphore_wait(
        barrier, 3 + 3 * has_below.astype(jnp.int32) + 3 * has_above.astype(jnp.int32)
    )

    def remote(k, j, src, dst, where):
        return pltpu.make_async_remote_copy(
            src_ref=src,
            dst_ref=dst,
            send_sem=send_sem.at[k, j],
            recv_sem=recv_sem.at[k, j],
            device_id=where,
            device_id_type=MESH,
        )

    inner = pl.ds(8, CY)

    def halo_copies(k):
        jobs = [
            (
                remote(k, Z_DOWN, u.at[k, :, 2:4, :, inner], u.at[k, :, CZ + 2 : CZ + 4, :, inner], {"gz": gz - 1}),
                has_below,
                has_above,
            ),
            (
                remote(k, Z_UP, u.at[k, :, CZ : CZ + 2, :, inner], u.at[k, :, 0:2, :, inner], {"gz": gz + 1}),
                has_above,
                has_below,
            ),
            (remote(k, Y_DOWN, sy.at[k, 0], ry.at[k, 1, :, :, :, 8:16], {"gy": down}), None, None),
            (remote(k, Y_UP, sy.at[k, 1], ry.at[k, 0, :, :, :, 8:16], {"gy": up}), None, None),
        ]
        for j, (a, b) in enumerate(CORNERS):
            jobs.append(
                (
                    remote(k, CORNER + j, cs.at[k, j], cr.at[k, j], {"gz": gz + a, "gy": beside[b]}),
                    has[a],
                    has[-a],
                )
            )
        return jobs

    def guarded(cond, act):
        if cond is None:
            act()
        else:
            pl.when(cond)(act)

    def u_row(c, z, l, y):
        return ((c * ZU + z + 2) * LT + l) * PY + y + 8

    def t_row(t, z, l, y):
        return ((t * ZT + z + 1) * LT + l) * PY + y + 8

    def pack(k):
        for side in range(2):
            for far in range(2):
                y = far if side == 0 else CY - 1 - far
                for c in range(3):
                    for l in range(LT):
                        sy[k, side, far, c, l] = flat[k][pl.ds(u_row(c, 0, l, y), CZ, stride=SPAN), :]
        for j, (a, b) in enumerate(CORNERS):
            z, y = (0 if a < 0 else CZ - 1), (0 if b < 0 else CY - 1)
            for c in range(3):
                cs[k, j, pl.ds(c * 8, LT), :] = flat[k][pl.ds(u_row(c, z, 0, y), LT, stride=PY), :]

    def unpack(k):
        for side in range(2):
            y = -1 if side == 0 else CY
            for c in range(3):
                for l in range(LT):
                    flat[k][pl.ds(u_row(c, 0, l, y), CZ, stride=SPAN), :] = ry[k, side, 0, c, l, 8:16, :]
        ry_flat = ry.at[k].reshape(2 * 2 * 3 * LT * 24, LANES)
        for j, (a, b) in enumerate(CORNERS):
            z, y, side = (-1 if a > 0 else CZ), (-1 if b > 0 else CY), (0 if b > 0 else 1)

            def place(j=j, z=z, y=y, side=side):
                for c in range(3):
                    rows = cr[k, j, pl.ds(c * 8, LT), :]
                    flat[k][pl.ds(u_row(c, z, 0, y), LT, stride=PY), :] = rows
                    at = ((side * 2 * 3 + c) * LT) * 24 + 8 + z
                    ry_flat[pl.ds(at, LT, stride=24), :] = rows

            pl.when(has[-a])(place)

    def turn(tiles):
        return [pltpu.roll(t, 1, 1) for t in tiles], [pltpu.roll(t, LANES - 1, 1) for t in tiles]

    def xdiff(turned, l):
        by_one, back_one = turned
        ahead = jnp.where(last_lane, back_one[(l + 1) % LT], back_one[l])
        behind = jnp.where(first_lane, by_one[(l - 1) % LT], by_one[l])
        return ahead - behind

    def stresses(load, weight, put):
        centre = [[load(c, l, 0, 0) for l in range(LT)] for c in range(3)]
        turned = [turn(tiles) for tiles in centre]
        for l in range(LT):
            d = [
                (
                    xdiff(turned[c], l),
                    load(c, l, 0, 1) - load(c, l, 0, -1),
                    load(c, l, 1, 0) - load(c, l, -1, 0),
                )
                for c in range(3)
            ]
            exy, exz, eyz = d[0][1] + d[1][0], d[0][2] + d[2][0], d[1][2] + d[2][1]
            squares = d[0][0] * d[0][0] + d[1][1] * d[1][1] + d[2][2] * d[2][2]
            squares = squares + 0.5 * (exy * exy + exz * exz + eyz * eyz)
            half = (0.5 * weight) * (squares * lax.rsqrt(jnp.maximum(squares, TINY)))
            full = half + half
            stress = {XX: (full, d[0][0]), YY: (full, d[1][1]), ZZ: (full, d[2][2])}
            stress.update({XY: (half, exy), XZ: (half, exz), YZ: (half, eyz)})
            put(l, lambda t, s=stress: s[t][0] * s[t][1], [centre[c][l] for c in range(3)], d)

    def stage(k):
        keep_u0, new = STAGES[k]
        weight = smag_coef * 0.5**0.5 * 0.5 * time_step * new
        jobs = halo_copies(k)
        pack(k)
        for copy, sends, _ in jobs:
            guarded(sends, copy.start)
        for copy, _, receives in jobs:
            guarded(receives, copy.wait_recv)
        unpack(k)

        def load_cell(z, h):
            def load(c, l, dz, dy):
                return layers[k][c * ZU + z + 2 + dz, pl.ds(l * PY + 8 + h + dy, 8), :]

            return load

        def own_layer(z, carry):
            for h in range(0, CY, 8):

                def put(l, stress, centre, d):
                    for t in range(6):
                        tau[t, z + 1, l, pl.ds(8 + h, 8), :] = stress(t)
                    for c in range(3):
                        adv = centre[0] * d[c][0] + centre[1] * d[c][1] + centre[2] * d[c][2]
                        value = centre[c] - (0.5 * time_step) * adv
                        if c == 0:
                            value = value + cnt[z, l, pl.ds(h, 8), :] * (centre[0] * jnp.abs(centre[0]))
                        if new != 1.0:
                            value = new * value
                        if keep_u0 != 0.0:
                            value = value + keep_u0 * u[0, c, z + 2, l, pl.ds(8 + h, 8), :]
                        acc[c, z, l, pl.ds(h, 8), :] = value

                stresses(load_cell(z, h), weight, put)
            return carry

        lax.fori_loop(0, CZ, own_layer, 0)

        for z, a in ((-1, -1), (CZ, 1)):
            masked = jnp.where(has[a], jnp.float32(weight), jnp.float32(0.0))
            for h in range(0, CY, 8):

                def put_layer(l, stress, centre, d):
                    for t in (XZ, YZ, ZZ):
                        tau[t, z + 1, l, pl.ds(8 + h, 8), :] = stress(t)

                stresses(load_cell(z, h), masked, put_layer)

        for side in range(2):
            y = -1 if side == 0 else CY
            outward = -1 if side == 0 else 1

            def load_row(c, l, dz, dy):
                if dy == 0:
                    return ry[k, side, 0, c, l, pl.ds(8 + dz, 8), :]
                if dy == outward:
                    return ry[k, side, 1, c, l, pl.ds(8, 8), :]
                return sy[k, side, 0, c, l]

            def put_row(l, stress, centre, d):
                for t in (XY, YY, YZ):
                    tau_flat[pl.ds(t_row(t, 0, l, y), CZ, stride=SPAN), :] = stress(t)

            stresses(load_row, weight, put_row)

        def advance(z, carry):
            for h in range(0, CY, 8):

                def at(t, l, dz=0, dy=0):
                    return tau_layers[t * ZT + z + 1 + dz, pl.ds(l * PY + 8 + h + dy, 8), :]

                for c, (tx, ty, tz) in enumerate(((XX, XY, XZ), (XY, YY, YZ), (XZ, YZ, ZZ))):
                    turned = turn([at(tx, l) for l in range(LT)])
                    for l in range(LT):
                        value = acc[c, z, l, pl.ds(h, 8), :] + xdiff(turned, l)
                        value = value + (at(ty, l, dy=1) - at(ty, l, dy=-1))
                        value = value + (at(tz, l, dz=1) - at(tz, l, dz=-1))
                        u[k + 1, c, z + 2, l, pl.ds(8 + h, 8), :] = value
            return carry

        lax.fori_loop(0, CZ, advance, 0)

        fringe = remote(k, BOX, u.at[k + 1, :, 2 : CZ + 2, 0, inner], arrived.at[k], {"box": 1})

        @pl.when(jnp.logical_not(is_main))
        def _():
            fringe.start()

        @pl.when(is_main)
        def _():
            fringe.wait_recv()

            def mix(z, carry):
                for c in range(3):
                    for h in range(0, CY, 8):
                        rows = pl.ds(8 + h, 8)
                        u[k + 1, c, z + 2, 0, rows, :] = 0.5 * (
                            u[k + 1, c, z + 2, 0, rows, :] + arrived[k, c, z, pl.ds(h, 8), :]
                        )
                return carry

            lax.fori_loop(0, CZ, mix, 0)

        return jobs, fringe

    sent = [stage(k) for k in range(3)]

    turned_in = lane >= r

    def rotate_out(z, carry):
        for c in range(3):
            for h in range(0, CY, 8):
                tiles = [
                    pltpu.roll(u[3, c, z + 2, (l - q) & (LT - 1), pl.ds(8 + h, 8), :], r, 1)
                    for l in range(-1, LT)
                ]
                for l in range(LT):
                    raw[c, z, l, pl.ds(h, 8), :] = jnp.where(turned_in, tiles[l + 1], tiles[l])
        return carry

    lax.fori_loop(0, CZ, rotate_out, 0)
    stores = [
        pltpu.make_async_copy(
            raw.at[:, :, l], out.at[0, :, :, :, pl.ds(l * LANES, LANES)], io_sem.at[l]
        )
        for l in range(LT)
    ]
    for copy in stores:
        copy.start()
    for jobs, fringe in sent:
        for copy, sends, _ in jobs:
            guarded(sends, copy.wait_send)
        pl.when(jnp.logical_not(is_main))(fringe.wait_send)
    for copy in stores:
        copy.wait()


def solution(mesh):
    nz, ny = mesh.shape["gz"], mesh.shape["gy"]

    def per_device(velocity, turbine_cells, turbine_count, fringe_start):
        f32 = jnp.float32
        return pl.pallas_call(
            functools.partial(kernel, nz, ny),
            out_shape=jax.ShapeDtypeStruct(velocity.shape, f32),
            in_specs=[
                pl.BlockSpec(memory_space=pltpu.SMEM),
                pl.BlockSpec(memory_space=pltpu.SMEM),
                pl.BlockSpec(memory_space=pltpu.VMEM),
                pl.BlockSpec(memory_space=pl.ANY),
            ],
            out_specs=pl.BlockSpec(memory_space=pl.ANY),
            scratch_shapes=[
                pltpu.VMEM((4, 3, ZU, LT, PY, LANES), f32),
                pltpu.VMEM((6, ZT, LT, PY, LANES), f32),
                pltpu.VMEM((3, CZ, LT, CY, LANES), f32),
                pltpu.VMEM((3, CZ, LT, CY, LANES), f32),
                pltpu.VMEM((CZ, LT, CY, LANES), f32),
                pltpu.VMEM((3, 2, 2, 3, LT, CZ, LANES), f32),
                pltpu.VMEM((3, 2, 2, 3, LT, CZ + 16, LANES), f32),
                pltpu.VMEM((3, 4, 24, LANES), f32),
                pltpu.VMEM((3, 4, 24, LANES), f32),
                pltpu.VMEM((3, 3, CZ, CY, LANES), f32),
                pltpu.SemaphoreType.DMA((LT,)),
                pltpu.SemaphoreType.DMA((3, COPIES)),
                pltpu.SemaphoreType.DMA((3, COPIES)),
            ],
            compiler_params=pltpu.CompilerParams(
                collective_id=0, has_side_effects=True, vmem_limit_bytes=48 << 20
            ),
        )(fringe_start, turbine_count, turbine_cells.reshape(1, -1), velocity)

    return jax.shard_map(
        per_device,
        mesh=mesh,
        in_specs=(P("box", None, "gz", "gy", None), P("gz", "gy", None), P("gz", "gy"), P()),
        out_specs=P("box", None, "gz", "gy", None),
        check_vma=False,
    )
```

time: 202 us -> 47.5 us (0.24)
  waiting for transfers between devices: 63.8 us -> 0 us
  starting transfers between devices: 63.4 us -> 0 us
  Pallas kernels: 0 us -> 43.9 us
  other arithmetic: 38.4 us -> 0 us
  local copies, waits for them, and re-layouts: 31.9 us -> 2.03 us
    ppermute x27 -> x0, waiting for transfers between devices: 63.8 us -> none  [the longest x3 57.3 us: shifted(): return lax.ppermute(value, axis, pairs)]
    ppermute x27 -> x0, starting transfers between devices: 63.4 us -> none  [the longest x12 33.6 us: extended(): lax.ppermute(lax.slice_in_dim(block, 0, width, axis=dim), axis, backward)]
    pallas_call x0 -> x1, Pallas kernels: none -> 43.9 us  [per_device(): pl.pallas_call(functools.partial(kernel, nz, ny), out_shape=jax.ShapeDtyp...]
    slice x34 -> x0, local copies, waits for them, and re-layouts: 12.9 us -> none  [the longest x9 6.38 us: extended(): lax.slice_in_dim(block, 0, width, axis=dim)]
    gather x3 -> x0, local copies, waits for them, and re-layouts: 12 us -> none  [drag_force(): vals = flat[cells]]
    mul x15 -> x0, other arithmetic: 11.8 us -> none  [the longest x3 4.77 us: xdiff(): return (jnp.roll(field, -1, -1) - jnp.roll(field, 1, -1)) * 0.5]
    scatter-add x6 -> x0, other arithmetic: 10.7 us -> none  [the longest x3 10.5 us: drag_force(): spread = jnp.zeros_like(flat).at[cells].add(force).reshape(ux.shape)]
    sub x3 -> x0, other arithmetic: 4.96 us -> none  [section_rates(): result = div - advection(field, grads)]
  transfers between devices with their start and end apart: 27 -> 0, of which waited for: 9 -> 0; matrix products, arithmetic and copies ran while one was open for 21% -> 0% of each run, Pallas kernels for 0% -> 0%
where the time goes in v1:
time: 47.5 us; the launch traced here: 47.2 us
  Pallas kernels  43.9 us (92%)
  local copies, waits for them, and re-layouts  2.03 us (4%)
  between operations  1.33 us (3%)
    pallas_call x1, Pallas kernels, per_device(): pl.pallas_call(functools.partial(kernel, nz, ny), out_shape=jax.ShapeDtyp...  43.9 us
    unnamed x5, local copies, waits for them, and re-layouts  2.03 us

profile of v1, /device:TPU:17, one launch (start us, length us, event | category | flops | bytes accessed | tf_op | source)
XLA Modules:
  0.0 47.2 jit_solution(6395033109653826703)
XLA Ops:
  0.7 0.0 copy-start.1
  1.3 0.0 copy-done.1
  1.3 0.0 copy-start
  1.3 1.1 %copy-done = f32[1,3,8,16,512]{4,3,2,1,0:T(8,128)S(1)} copy-done((f32[1,3,8,16,512]{4,3,2,1,0:T(8,128)S(1)}, f32[1,3,8,16,512]{4,3,2,1,0:T(8,128)}, u32[]{:S(2)}) %copy-start) | copy-done | bytes 786456
  2.5 43.9 %shard_map.46 = f32[1,3,8,16,512]{4,3,2,1,0:T(8,128)S(1)} custom-call(s32[1]{0:T(128)S(6)} %copy.7.start, s32[1,1]{1,0:T(1,128)S(6)} %copy.6.count, s32[1,512]{1,0:T(1,128)S(1)} %bitcast.1, f32[1,3,8,16,512]{4,3,2,1,0:T(8,128)S(1)} %copy-done), custom_call_target="tpu_custom_call" | custom-call | tf_op jit(solution)/shard_map/pallas_call | solution.py:389
  46.3 0.9 %copy.8 = f32[1,3,8,16,512]{4,3,2,1,0:T(8,128)} copy(f32[1,3,8,16,512]{4,3,2,1,0:T(8,128)S(1)} %shard_map.46) | data formatting | bytes 1572864
Async XLA Ops:
  0.7 0.7 %copy-start.1 = (s32[1,1,512]{2,1,0:T(1,128)S(1)}, s32[1,1,512]{2,1,0:T(1,128)}, u32[]{:S(2)}) copy-start(s32[1,1,512]{2,1,0:T(1,128)} %param.5) | copy-start | bytes 6148
  1.3 1.1 %copy-start = (f32[1,3,8,16,512]{4,3,2,1,0:T(8,128)S(1)}, f32[1,3,8,16,512]{4,3,2,1,0:T(8,128)}, u32[]{:S(2)}) copy-start(f32[1,3,8,16,512]{4,3,2,1,0:T(8,128)} %vel.1) | copy-start | bytes 2359300

commit v2 on v1

v2 whole, which is shorter than its diff:
```python
import functools

import jax
import jax.numpy as jnp
from jax import lax
from jax.experimental import pallas as pl
from jax.experimental.pallas import tpu as pltpu
from jax.sharding import PartitionSpec as P

MESH = pl.DeviceIdType.MESH
CZ, CY, NX = 8, 16, 512
LANES = 128
LT = NX // LANES
PY = 32
ZU = CZ + 4
ZT = CZ + 2
SPAN = LT * PY

smag_coef = 0.1024
drag_coef = 0.665
time_step = 0.2
TINY = 1e-37
XX, YY, ZZ, XY, XZ, YZ = range(6)
STAGES = ((0.0, 1.0), (0.75, 0.25), (1.0 / 3.0, 2.0 / 3.0))
CORNERS = ((-1, -1), (-1, 1), (1, -1), (1, 1))
Z_DOWN, Z_UP, Y_DOWN, Y_UP, CORNER, BOX = 0, 1, 2, 3, 4, 8
COPIES = 9
SEND_ORDER = (Y_DOWN, Y_UP, CORNER, CORNER + 1, CORNER + 2, CORNER + 3, Z_DOWN, Z_UP)


def kernel(
    nz, ny, start, count, cells, vel, out, u, tau, acc, raw, cnt, own, slots_of, ry, arrived, io_sem, send_sem, recv_sem
):
    gz, gy, box = lax.axis_index("gz"), lax.axis_index("gy"), lax.axis_index("box")
    up, down = lax.rem(gy + 1, ny), lax.rem(gy + ny - 1, ny)
    has_below, has_above = gz > 0, gz < nz - 1
    is_main = box == 1
    has = {-1: has_below, 1: has_above}
    beside = {-1: down, 1: up}

    loads = [
        pltpu.make_async_copy(
            vel.at[0, :, :, :, pl.ds(l * LANES, LANES)], raw.at[:, :, l], io_sem.at[l]
        )
        for l in range(LT)
    ]
    for copy in loads:
        copy.start()

    barrier = pltpu.get_barrier_semaphore()

    def greet(where):
        pl.semaphore_signal(barrier, inc=1, device_id=where, device_id_type=MESH)

    greet({"gy": down})
    greet({"gy": up})
    greet({"box": 1 - box})
    for a in (-1, 1):

        @pl.when(has[a])
        def _(a=a):
            greet({"gz": gz + a})
            greet({"gz": gz + a, "gy": down})
            greet({"gz": gz + a, "gy": up})

    lane = lax.broadcasted_iota(jnp.int32, (8, LANES), 1)
    first_lane, last_lane = lane == 0, lane == LANES - 1

    flat = [u.at[k].reshape(3 * ZU * SPAN, LANES) for k in range(4)]
    layers = [u.at[k].reshape(3 * ZU, SPAN, LANES) for k in range(4)]
    ry_layers = [ry.at[k].reshape(2 * 3 * ZT, 2 * LT, LANES) for k in range(3)]
    ry_flat = [ry.at[k].reshape(2 * 3 * ZT * 2 * LT, LANES) for k in range(3)]
    acc_flat = acc.reshape(3 * CZ * LT * CY, LANES)
    tau_flat = tau.reshape(6 * ZT * SPAN, LANES)
    tau_layers = tau.reshape(6 * ZT, SPAN, LANES)

    zeros = jnp.zeros((8, LANES), jnp.float32)
    for a, at in ((-1, 0), (1, CZ + 2)):

        @pl.when(jnp.logical_not(has[a]))
        def _(a=a, at=at):
            def clear(k):
                for c in range(3):
                    for z in range(2):
                        for l in range(LT):
                            for r in range(0, PY, 8):
                                u[k, c, at + z, l, pl.ds(r, 8), :] = zeros
                for side in range(2):
                    for c in range(3):
                        ry_layers[k][(side * 3 + c) * ZT + (0 if a < 0 else ZT - 1), :, :] = zeros

            for k in range(3):
                clear(k)

    s = start[0]
    q = lax.shift_right_logical(s, 7)
    r = s & (LANES - 1)
    left = (LANES - r) & (LANES - 1)
    keep = lane < LANES - r
    for copy in loads:
        copy.wait()

    def rotate_in(z, carry):
        for c in range(3):
            for h in range(0, CY, 8):
                tiles = [
                    pltpu.roll(raw[c, z, (l + q) & (LT - 1), pl.ds(h, 8), :], left, 1)
                    for l in range(LT)
                ]
                for l in range(LT):
                    u[0, c, z + 2, l, pl.ds(8 + h, 8), :] = jnp.where(
                        keep, tiles[l], tiles[(l + 1) % LT]
                    )
        return carry

    lax.fori_loop(0, CZ, rotate_in, 0)

    pl.semaphore_wait(
        barrier, 3 + 3 * has_below.astype(jnp.int32) + 3 * has_above.astype(jnp.int32)
    )

    def remote(k, j, src, dst, where):
        return pltpu.make_async_remote_copy(
            src_ref=src,
            dst_ref=dst,
            send_sem=send_sem.at[k, j],
            recv_sem=recv_sem.at[k, j],
            device_id=where,
            device_id_type=MESH,
        )

    inner = pl.ds(8, CY)
    own_z = pl.ds(2, CZ)

    def halo_copies(k):
        jobs = [
            (
                remote(k, Z_DOWN, u.at[k, :, 2:4, :, inner], u.at[k, :, CZ + 2 : CZ + 4, :, inner], {"gz": gz - 1}),
                has_below,
                has_above,
            ),
            (
                remote(k, Z_UP, u.at[k, :, CZ : CZ + 2, :, inner], u.at[k, :, 0:2, :, inner], {"gz": gz + 1}),
                has_above,
                has_below,
            ),
            (remote(k, Y_DOWN, u.at[k, :, own_z, :, 8:10], ry.at[k, 1, :, 1 : CZ + 1], {"gy": down}), None, None),
            (
                remote(k, Y_UP, u.at[k, :, own_z, :, 6 + CY : 8 + CY], ry.at[k, 0, :, 1 : CZ + 1], {"gy": up}),
                None,
                None,
            ),
        ]
        for j, (a, b) in enumerate(CORNERS):
            z, y = (2 if a < 0 else CZ + 1), (8 if b < 0 else 7 + CY)
            side, near = (1, 0) if b < 0 else (0, 1)
            jobs.append(
                (
                    remote(
                        k,
                        CORNER + j,
                        u.at[k, :, z, :, y : y + 1],
                        ry.at[k, side, :, ZT - 1 if a < 0 else 0, :, near : near + 1],
                        {"gz": gz + a, "gy": beside[b]},
                    ),
                    has[a],
                    has[-a],
                )
            )
        return jobs

    def guarded(cond, act):
        if cond is None:
            act()
        else:
            pl.when(cond)(act)

    def u_row(c, z, l, y):
        return ((c * ZU + z + 2) * LT + l) * PY + y + 8

    def t_row(t, z, l, y):
        return ((t * ZT + z + 1) * LT + l) * PY + y + 8

    def a_row(c, z, l, y):
        return ((c * CZ + z) * LT + l) * CY + y

    def r_row(side, c, z, l, far):
        return (((side * 3 + c) * ZT + z + 1) * LT + l) * 2 + (1 - far if side == 0 else far)

    def edge(side, far):
        return far if side == 0 else CY - 1 - far

    def pack_own(k):
        for side in range(2):
            for far in range(2):
                for c in range(3):
                    for l in range(LT):
                        own[k, side, far, c, l, 8:16, :] = flat[k][
                            pl.ds(u_row(c, 0, l, edge(side, far)), CZ, stride=SPAN), :
                        ]

    def place_rows(k):
        for z in (-1, 0, CZ - 1, CZ):
            for side in range(2):
                y = -1 if side == 0 else CY
                for c in range(3):
                    for l in range(LT):
                        flat[k][pl.ds(u_row(c, z, l, y), 1), :] = ry_flat[k][pl.ds(r_row(side, c, z, l, 0), 1), :]

    def turn(tiles):
        return [pltpu.roll(t, 1, 1) for t in tiles], [pltpu.roll(t, LANES - 1, 1) for t in tiles]

    def xdiff(turned, l):
        by_one, back_one = turned
        ahead = jnp.where(last_lane, back_one[(l + 1) % LT], back_one[l])
        behind = jnp.where(first_lane, by_one[(l - 1) % LT], by_one[l])
        return ahead - behind

    def stresses(load, weight, wanted, put, base=None, finish=None):
        centre = [[load(c, l, 0, 0) for l in range(LT)] for c in range(3)]
        turned = [turn(tiles) for tiles in centre]
        along_x = [[None] * LT for _ in range(3)]
        start_from = [[None] * LT for _ in range(3)]
        for l in range(LT):
            d = [
                (
                    xdiff(turned[c], l),
                    load(c, l, 0, 1) - load(c, l, 0, -1),
                    load(c, l, 1, 0) - load(c, l, -1, 0),
                )
                for c in range(3)
            ]
            exy, exz, eyz = d[0][1] + d[1][0], d[0][2] + d[2][0], d[1][2] + d[2][1]
            squares = d[0][0] * d[0][0] + d[1][1] * d[1][1] + d[2][2] * d[2][2]
            squares = squares + 0.5 * (exy * exy + exz * exz + eyz * eyz)
            half = (0.5 * weight) * (squares * lax.rsqrt(jnp.maximum(squares, TINY)))
            full = half + half
            factors = {XX: (full, d[0][0]), YY: (full, d[1][1]), ZZ: (full, d[2][2])}
            factors.update({XY: (half, exy), XZ: (half, exz), YZ: (half, eyz)})
            stress = {t: factors[t][0] * factors[t][1] for t in wanted}
            for t in wanted:
                if t != XX:
                    put(t, l, stress[t])
            if base is not None:
                for c, t in enumerate((XX, XY, XZ)):
                    along_x[c][l] = stress[t]
                    start_from[c][l] = base(c, l, [centre[i][l] for i in range(3)], d[c])
        if base is not None:
            for c in range(3):
                turned = turn(along_x[c])
                for l in range(LT):
                    finish(c, l, start_from[c][l] + xdiff(turned, l))

    def count_slots():
        flat_cells = cells[...]
        row = lax.shift_right_logical(flat_cells, 9)
        col = (flat_cells - s) & (NX - 1)
        slots = cells.shape[1]
        live = lax.broadcasted_iota(jnp.int32, (1, slots), 1) < count[0, 0]
        row = jnp.where(live, row, -1)
        rows = lax.broadcasted_iota(jnp.int32, (CZ * CY, slots), 0)
        cols = lax.broadcasted_iota(jnp.int32, (NX, slots), 0)
        pick_row = jnp.where(rows == row, 1.0, 0.0).astype(jnp.bfloat16)
        pick_col = jnp.where(cols == col, 1.0, 0.0).astype(jnp.bfloat16)
        times = lax.dot_general(
            pick_row, pick_col, (((1,), (1,)), ((), ())), preferred_element_type=jnp.float32
        )
        times = times * jnp.where(is_main, -drag_coef * time_step, 0.0)
        for l in range(LT):
            cnt[:, l] = times[:, l * LANES : (l + 1) * LANES].reshape(CZ, CY, LANES)
        cnt_flat = cnt.reshape(CZ * LT * CY, LANES)
        for side in range(2):
            for l in range(LT):
                slots_of[side, l] = cnt_flat[pl.ds(l * CY + edge(side, 0), CZ, stride=LT * CY), :]

    def stage(k):
        keep_u0, new = STAGES[k]
        weight = smag_coef * 0.5**0.5 * 0.5 * time_step * new
        jobs = halo_copies(k)
        for j in SEND_ORDER:
            copy, sends, _ = jobs[j]
            guarded(sends, copy.start)
        if k == 0:
            count_slots()

        def rate(c, centre, d, times, before):
            adv = centre[0] * d[0] + centre[1] * d[1] + centre[2] * d[2]
            value = centre[c] - (0.5 * time_step) * adv
            if c == 0:
                value = value + times() * (centre[0] * jnp.abs(centre[0]))
            if new != 1.0:
                value = new * value
            if keep_u0 != 0.0:
                value = value + keep_u0 * before()
            return value

        def load_cell(z, h):
            def load(c, l, dz, dy):
                return layers[k][c * ZU + z + 2 + dz, pl.ds(l * PY + 8 + h + dy, 8), :]

            return load

        def own_layer(z):
            for h in range(0, CY, 8):

                def put(t, l, value):
                    tau[t, z + 1, l, pl.ds(8 + h, 8), :] = value

                def base(c, l, centre, d):
                    return rate(
                        c,
                        centre,
                        d,
                        lambda: cnt[z, l, pl.ds(h, 8), :],
                        lambda: u[0, c, z + 2, l, pl.ds(8 + h, 8), :],
                    )

                def finish(c, l, value):
                    acc[c, z, l, pl.ds(h, 8), :] = value

                stresses(load_cell(z, h), weight, range(6), put, base, finish)

        def inside(z, carry):
            own_layer(z)
            return carry

        pack_own(k)
        lax.fori_loop(1, CZ - 1, inside, 0)
        for j in (Y_DOWN, Y_UP):
            jobs[j][0].wait_recv()

        for side in range(2):
            y = edge(side, 0)
            outward = -1 if side == 0 else 1

            def load_edge(c, l, dz, dy):
                if dy == 0:
                    return own[k, side, 0, c, l, pl.ds(8 + dz, 8), :]
                if dy == outward:
                    return ry_flat[k][pl.ds(r_row(side, c, 0, l, 0), CZ, stride=2 * LT), :]
                return own[k, side, 1, c, l, 8:16, :]

            def put_edge(t, l, value):
                tau_flat[pl.ds(t_row(t, 0, l, y), CZ, stride=SPAN), :] = value

            def base_edge(c, l, centre, d):
                return rate(c, centre, d, lambda: slots_of[side, l], lambda: own[0, side, 0, c, l, 8:16, :])

            def finish_edge(c, l, value):
                acc_flat[pl.ds(a_row(c, 0, l, y), CZ, stride=LT * CY), :] = value

            stresses(load_edge, weight, range(6), put_edge, base_edge, finish_edge)

        for j in (CORNER, CORNER + 1, CORNER + 2, CORNER + 3, Z_DOWN, Z_UP):
            copy, _, receives = jobs[j]
            guarded(receives, copy.wait_recv)
        place_rows(k)
        own_layer(0)
        own_layer(CZ - 1)

        for z, a in ((-1, -1), (CZ, 1)):
            masked = jnp.where(has[a], jnp.float32(weight), jnp.float32(0.0))
            for h in range(0, CY, 8):

                def put_layer(t, l, value):
                    tau[t, z + 1, l, pl.ds(8 + h, 8), :] = value

                stresses(load_cell(z, h), masked, (XZ, YZ, ZZ), put_layer)

        for side in range(2):
            y = -1 if side == 0 else CY
            outward = -1 if side == 0 else 1

            def load_row(c, l, dz, dy):
                if dy == 0:
                    return ry_flat[k][pl.ds(r_row(side, c, dz, l, 0), CZ, stride=2 * LT), :]
                if dy == outward:
                    return ry_flat[k][pl.ds(r_row(side, c, 0, l, 1), CZ, stride=2 * LT), :]
                return own[k, side, 0, c, l, 8:16, :]

            def put_row(t, l, value):
                tau_flat[pl.ds(t_row(t, 0, l, y), CZ, stride=SPAN), :] = value

            stresses(load_row, weight, (XY, YY, YZ), put_row)

        def advance(tiles, z, carry):
            for h in range(0, CY, 8):

                def at(t, l, dz=0, dy=0):
                    return tau_layers[t * ZT + z + 1 + dz, pl.ds(l * PY + 8 + h + dy, 8), :]

                for c, (ty, tz) in enumerate(((XY, XZ), (YY, YZ), (YZ, ZZ))):
                    for l in tiles:
                        value = acc[c, z, l, pl.ds(h, 8), :] + (at(ty, l, dy=1) - at(ty, l, dy=-1))
                        value = value + (at(tz, l, dz=1) - at(tz, l, dz=-1))
                        u[k + 1, c, z + 2, l, pl.ds(8 + h, 8), :] = value
            return carry

        fringe = remote(k, BOX, u.at[k + 1, :, own_z, 0, inner], arrived.at[k], {"box": 1})
        lax.fori_loop(0, CZ, functools.partial(advance, (0,)), 0)

        @pl.when(jnp.logical_not(is_main))
        def _():
            fringe.start()

        lax.fori_loop(0, CZ, functools.partial(advance, (1, 2, 3)), 0)

        @pl.when(is_main)
        def _():
            fringe.wait_recv()

            def mix(z, carry):
                for c in range(3):
                    for h in range(0, CY, 8):
                        rows = pl.ds(8 + h, 8)
                        u[k + 1, c, z + 2, 0, rows, :] = 0.5 * (
                            u[k + 1, c, z + 2, 0, rows, :] + arrived[k, c, z, pl.ds(h, 8), :]
                        )
                return carry

            lax.fori_loop(0, CZ, mix, 0)

        return jobs, fringe

    sent = [stage(k) for k in range(3)]

    turned_in = lane >= r

    def rotate_out(z, carry):
        for c in range(3):
            for h in range(0, CY, 8):
                tiles = [
                    pltpu.roll(u[3, c, z + 2, (l - q) & (LT - 1), pl.ds(8 + h, 8), :], r, 1)
                    for l in range(-1, LT)
                ]
                for l in range(LT):
                    out[0, c, z, pl.ds(h, 8), pl.ds(l * LANES, LANES)] = jnp.where(
                        turned_in, tiles[l + 1], tiles[l]
                    )
        return carry

    lax.fori_loop(0, CZ, rotate_out, 0)
    for jobs, fringe in sent:
        for copy, sends, _ in jobs:
            guarded(sends, copy.wait_send)
        pl.when(jnp.logical_not(is_main))(fringe.wait_send)


def solution(mesh):
    nz, ny = mesh.shape["gz"], mesh.shape["gy"]

    def per_device(velocity, turbine_cells, turbine_count, fringe_start):
        f32 = jnp.float32
        return pl.pallas_call(
            functools.partial(kernel, nz, ny),
            out_shape=jax.ShapeDtypeStruct(velocity.shape, f32),
            in_specs=[
                pl.BlockSpec(memory_space=pltpu.SMEM),
                pl.BlockSpec(memory_space=pltpu.SMEM),
                pl.BlockSpec(memory_space=pltpu.VMEM),
                pl.BlockSpec(memory_space=pltpu.MemorySpace.HBM),
            ],
            out_specs=pl.BlockSpec(memory_space=pltpu.VMEM),
            scratch_shapes=[
                pltpu.VMEM((4, 3, ZU, LT, PY, LANES), f32),
                pltpu.VMEM((6, ZT, LT, PY, LANES), f32),
                pltpu.VMEM((3, CZ, LT, CY, LANES), f32),
                pltpu.VMEM((3, CZ, LT, CY, LANES), f32),
                pltpu.VMEM((CZ, LT, CY, LANES), f32),
                pltpu.VMEM((3, 2, 2, 3, LT, CZ + 16, LANES), f32),
                pltpu.VMEM((2, LT, CZ, LANES), f32),
                pltpu.VMEM((3, 2, 3, ZT, LT, 2, LANES), f32),
                pltpu.VMEM((3, 3, CZ, CY, LANES), f32),
                pltpu.SemaphoreType.DMA((LT,)),
                pltpu.SemaphoreType.DMA((3, COPIES)),
                pltpu.SemaphoreType.DMA((3, COPIES)),
            ],
            compiler_params=pltpu.CompilerParams(
                collective_id=0, has_side_effects=True, vmem_limit_bytes=48 << 20
            ),
        )(fringe_start, turbine_count, turbine_cells.reshape(1, -1), velocity)

    return jax.shard_map(
        per_device,
        mesh=mesh,
        in_specs=(P("box", None, "gz", "gy", None), P("gz", "gy", None), P("gz", "gy"), P()),
        out_specs=P("box", None, "gz", "gy", None),
        check_vma=False,
    )
```

time: 47.5 us -> 41.9 us (0.88)
  Pallas kernels: 43.9 us -> 38.4 us
    pallas_call x1, Pallas kernels: 43.9 us -> 38.4 us  [per_device(): pl.pallas_call(functools.partial(kernel, nz, ny), out_shape=jax.ShapeDtyp...]
where the time goes in v2:
time: 41.9 us; the launch traced here: 41.8 us
  Pallas kernels  38.4 us (92%)
  local copies, waits for them, and re-layouts  2.03 us (5%)
  between operations  1.33 us (3%)
    pallas_call x1, Pallas kernels, per_device(): pl.pallas_call(functools.partial(kernel, nz, ny), out_shape=jax.ShapeDtyp...  38.4 us
    unnamed x5, local copies, waits for them, and re-layouts  2.03 us

profile of v2, /device:TPU:17, one launch (start us, length us, event | category | flops | bytes accessed | tf_op | source)
XLA Modules:
  0.0 41.8 jit_solution(2165345822152063849)
XLA Ops:
  0.7 0.0 copy-start.1
  1.3 0.0 copy-done.1
  1.3 0.0 copy-start
  1.3 1.1 %copy-done = f32[1,3,8,16,512]{4,3,2,1,0:T(8,128)S(1)} copy-done((f32[1,3,8,16,512]{4,3,2,1,0:T(8,128)S(1)}, f32[1,3,8,16,512]{4,3,2,1,0:T(8,128)}, u32[]{:S(2)}) %copy-start) | copy-done | bytes 786456
  2.5 38.4 %shard_map.46 = f32[1,3,8,16,512]{4,3,2,1,0:T(8,128)S(1)} custom-call(s32[1]{0:T(128)S(6)} %copy.7.start, s32[1,1]{1,0:T(1,128)S(6)} %copy.6.count, s32[1,512]{1,0:T(1,128)S(1)} %bitcast.1, f32[1,3,8,16,512]{4,3,2,1,0:T(8,128)S(1)} %copy-done), custom_call_target="tpu_custom_call" | custom-call | tf_op jit(solution)/shard_map/pallas_call | solution.py:454
  40.9 0.9 %copy.8 = f32[1,3,8,16,512]{4,3,2,1,0:T(8,128)} copy(f32[1,3,8,16,512]{4,3,2,1,0:T(8,128)S(1)} %shard_map.46) | data formatting | bytes 1572864
Async XLA Ops:
  0.7 0.7 %copy-start.1 = (s32[1,1,512]{2,1,0:T(1,128)S(1)}, s32[1,1,512]{2,1,0:T(1,128)}, u32[]{:S(2)}) copy-start(s32[1,1,512]{2,1,0:T(1,128)} %param.5) | copy-start | bytes 6148
  1.3 1.1 %copy-start = (f32[1,3,8,16,512]{4,3,2,1,0:T(8,128)S(1)}, f32[1,3,8,16,512]{4,3,2,1,0:T(8,128)}, u32[]{:S(2)}) copy-start(f32[1,3,8,16,512]{4,3,2,1,0:T(8,128)} %vel.1) | copy-start | bytes 2359300

commit v3 on v2

--- a/solution.py
+++ b/solution.py
@@ -23,13 +23,15 @@
 XX, YY, ZZ, XY, XZ, YZ = range(6)
 STAGES = ((0.0, 1.0), (0.75, 0.25), (1.0 / 3.0, 2.0 / 3.0))
 CORNERS = ((-1, -1), (-1, 1), (1, -1), (1, 1))
-Z_DOWN, Z_UP, Y_DOWN, Y_UP, CORNER, BOX = 0, 1, 2, 3, 4, 8
-COPIES = 9
-SEND_ORDER = (Y_DOWN, Y_UP, CORNER, CORNER + 1, CORNER + 2, CORNER + 3, Z_DOWN, Z_UP)
+ROWS, LAYERS, FAR_LAYERS = (0, 1), (2, 3), (4, 5)
+CORNER, BOX = 6, 10
+DIAGONALS = tuple(range(CORNER, CORNER + 4))
+COPIES = 15
+SEND_ORDER = DIAGONALS + ROWS + LAYERS + FAR_LAYERS
 
 
 def kernel(
-    nz, ny, start, count, cells, vel, out, u, tau, acc, raw, cnt, own, slots_of, ry, arrived, io_sem, send_sem, recv_sem
+    nz, ny, start, count, cells, vel, out, u, tau, acc, cnt, own, slots_of, ry, early, arrived, send_sem, recv_sem
 ):
     gz, gy, box = lax.axis_index("gz"), lax.axis_index("gy"), lax.axis_index("box")
     up, down = lax.rem(gy + 1, ny), lax.rem(gy + ny - 1, ny)
@@ -38,15 +40,6 @@
     has = {-1: has_below, 1: has_above}
     beside = {-1: down, 1: up}
 
-    loads = [
-        pltpu.make_async_copy(
-            vel.at[0, :, :, :, pl.ds(l * LANES, LANES)], raw.at[:, :, l], io_sem.at[l]
-        )
-        for l in range(LT)
-    ]
-    for copy in loads:
-        copy.start()
-
     barrier = pltpu.get_barrier_semaphore()
 
     def greet(where):
@@ -74,46 +67,32 @@
     tau_flat = tau.reshape(6 * ZT * SPAN, LANES)
     tau_layers = tau.reshape(6 * ZT, SPAN, LANES)
 
-    zeros = jnp.zeros((8, LANES), jnp.float32)
-    for a, at in ((-1, 0), (1, CZ + 2)):
-
-        @pl.when(jnp.logical_not(has[a]))
-        def _(a=a, at=at):
-            def clear(k):
-                for c in range(3):
-                    for z in range(2):
-                        for l in range(LT):
-                            for r in range(0, PY, 8):
-                                u[k, c, at + z, l, pl.ds(r, 8), :] = zeros
-                for side in range(2):
-                    for c in range(3):
-                        ry_layers[k][(side * 3 + c) * ZT + (0 if a < 0 else ZT - 1), :, :] = zeros
-
-            for k in range(3):
-                clear(k)
-
     s = start[0]
     q = lax.shift_right_logical(s, 7)
     r = s & (LANES - 1)
     left = (LANES - r) & (LANES - 1)
     keep = lane < LANES - r
-    for copy in loads:
-        copy.wait()
+    q_lanes = jnp.zeros((8, LANES), jnp.int32) + q
+    by_one_tile, by_two_tiles = (q_lanes & 1) == 1, (q_lanes & 2) == 2
+
+    def turned_tiles(tiles, way):
+        tiles = [jnp.where(by_one_tile, tiles[(l + way) % LT], tiles[l]) for l in range(LT)]
+        return [jnp.where(by_two_tiles, tiles[(l + 2) % LT], tiles[l]) for l in range(LT)]
 
     def rotate_in(z, carry):
         for c in range(3):
             for h in range(0, CY, 8):
-                tiles = [
-                    pltpu.roll(raw[c, z, (l + q) & (LT - 1), pl.ds(h, 8), :], left, 1)
-                    for l in range(LT)
-                ]
+                tiles = turned_tiles(
+                    [vel[0, c, z, pl.ds(h, 8), l * LANES : (l + 1) * LANES] for l in range(LT)], 1
+                )
+                tiles = [pltpu.roll(t, left, 1) for t in tiles]
                 for l in range(LT):
                     u[0, c, z + 2, l, pl.ds(8 + h, 8), :] = jnp.where(
                         keep, tiles[l], tiles[(l + 1) % LT]
                     )
         return carry
 
-    lax.fori_loop(0, CZ, rotate_in, 0)
+    lax.fori_loop(0, CZ, rotate_in, 0, unroll=4)
 
     pl.semaphore_wait(
         barrier, 3 + 3 * has_below.astype(jnp.int32) + 3 * has_above.astype(jnp.int32)
@@ -134,23 +113,20 @@
 
     def halo_copies(k):
         jobs = [
-            (
-                remote(k, Z_DOWN, u.at[k, :, 2:4, :, inner], u.at[k, :, CZ + 2 : CZ + 4, :, inner], {"gz": gz - 1}),
-                has_below,
-                has_above,
-            ),
-            (
-                remote(k, Z_UP, u.at[k, :, CZ : CZ + 2, :, inner], u.at[k, :, 0:2, :, inner], {"gz": gz + 1}),
-                has_above,
-                has_below,
-            ),
-            (remote(k, Y_DOWN, u.at[k, :, own_z, :, 8:10], ry.at[k, 1, :, 1 : CZ + 1], {"gy": down}), None, None),
-            (
-                remote(k, Y_UP, u.at[k, :, own_z, :, 6 + CY : 8 + CY], ry.at[k, 0, :, 1 : CZ + 1], {"gy": up}),
-                None,
-                None,
-            ),
+            (remote(k, 0, u.at[k, :, own_z, :, 8:10], ry.at[k, 1, :, 1 : CZ + 1], {"gy": down}), None, None),
+            (remote(k, 1, u.at[k, :, own_z, :, 6 + CY : 8 + CY], ry.at[k, 0, :, 1 : CZ + 1], {"gy": up}), None, None),
         ]
+        for far in range(2):
+            for a, src, dst in ((-1, 2 + far, CZ + 2 + far), (1, CZ + 1 - far, 1 - far)):
+                jobs.append(
+                    (
+                        remote(
+                            k, len(jobs), u.at[k, :, src, :, inner], u.at[k, :, dst, :, inner], {"gz": gz + a}
+                        ),
+                        has[a],
+                        has[-a],
+                    )
+                )
         for j, (a, b) in enumerate(CORNERS):
             z, y = (2 if a < 0 else CZ + 1), (8 if b < 0 else 7 + CY)
             side, near = (1, 0) if b < 0 else (0, 1)
@@ -199,13 +175,22 @@
                             pl.ds(u_row(c, 0, l, edge(side, far)), CZ, stride=SPAN), :
                         ]
 
-    def place_rows(k):
-        for z in (-1, 0, CZ - 1, CZ):
+    def place_corners(k):
+        for z in (-1, CZ):
             for side in range(2):
                 y = -1 if side == 0 else CY
                 for c in range(3):
                     for l in range(LT):
                         flat[k][pl.ds(u_row(c, z, l, y), 1), :] = ry_flat[k][pl.ds(r_row(side, c, z, l, 0), 1), :]
+
+    def pad_own(k):
+        for side in range(2):
+            for z in (-1, CZ):
+                for c in range(3):
+                    for l in range(LT):
+                        own[k, side, 0, c, l, 8 + z : 9 + z, :] = flat[k][
+                            pl.ds(u_row(c, z, l, edge(side, 0)), 1), :
+                        ]
 
     def turn(tiles):
         return [pltpu.roll(t, 1, 1) for t in tiles], [pltpu.roll(t, LANES - 1, 1) for t in tiles]
@@ -251,6 +236,25 @@
                 for l in range(LT):
                     finish(c, l, start_from[c][l] + xdiff(turned, l))
 
+    def clear_outside():
+        zeros = jnp.zeros((8, LANES), jnp.float32)
+        for a, at in ((-1, 0), (1, CZ + 2)):
+
+            @pl.when(jnp.logical_not(has[a]))
+            def _(a=a, at=at):
+                def clear(k):
+                    for c in range(3):
+                        for z in range(2):
+                            for l in range(LT):
+                                for r in range(0, PY, 8):
+                                    u[k, c, at + z, l, pl.ds(r, 8), :] = zeros
+                    for side in range(2):
+                        for c in range(3):
+                            ry_layers[k][(side * 3 + c) * ZT + (0 if a < 0 else ZT - 1), :, :] = zeros
+
+                for k in range(3):
+                    clear(k)
+
     def count_slots():
         flat_cells = cells[...]
         row = lax.shift_right_logical(flat_cells, 9)
@@ -281,6 +285,7 @@
             copy, sends, _ = jobs[j]
             guarded(sends, copy.start)
         if k == 0:
+            clear_outside()
             count_slots()
 
         def rate(c, centre, d, times, before):
@@ -320,15 +325,73 @@
 
                 stresses(load_cell(z, h), weight, range(6), put, base, finish)
 
+        def advance(tiles, z, put):
+            for h in range(0, CY, 8):
+
+                def at(t, l, dz=0, dy=0):
+                    return tau_layers[t * ZT + z + 1 + dz, pl.ds(l * PY + 8 + h + dy, 8), :]
+
+                for c, (ty, tz) in enumerate(((XY, XZ), (YY, YZ), (YZ, ZZ))):
+                    for l in tiles:
+                        value = acc[c, z, l, pl.ds(h, 8), :] + (at(ty, l, dy=1) - at(ty, l, dy=-1))
+                        put(c, z, h, l, value + (at(tz, l, dz=1) - at(tz, l, dz=-1)))
+
+        def arrive(which):
+            for j in which:
+                copy, _, receives = jobs[j]
+                guarded(receives, copy.wait_recv)
+
+        middle = pl.ds(2, CY - 4)
+        pieces = [
+            (early.at[k, :, z : z + n, middle], arrived.at[k, :, z : z + n, middle])
+            for z, n in ((2, CZ - 4), (0, 2), (CZ - 2, 2))
+        ]
+        for y in (0, CY - 2):
+            pieces.append((u.at[k + 1, :, own_z, 0, y + 8 : y + 10], arrived.at[k, :, :, y : y + 2]))
+        fringe = [remote(k, BOX + i, src, dst, {"box": 1}) for i, (src, dst) in enumerate(pieces)]
+
         def inside(z, carry):
             own_layer(z)
             return carry
 
         pack_own(k)
         lax.fori_loop(1, CZ - 1, inside, 0)
-        for j in (Y_DOWN, Y_UP):
-            jobs[j][0].wait_recv()
-
+        def put_early(c, z, h, l, value):
+            early[k, c, z, pl.ds(h, 8), :] = value
+
+        def advance_early(z, carry):
+            advance((0,), z, put_early)
+            return carry
+
+        @pl.when(jnp.logical_not(is_main))
+        def _():
+            lax.fori_loop(2, CZ - 2, advance_early, 0)
+            fringe[0].start()
+
+        arrive(LAYERS)
+        own_layer(0)
+        own_layer(CZ - 1)
+        pad_own(k)
+        arrive(DIAGONALS + FAR_LAYERS)
+        place_corners(k)
+        for z, a in ((-1, -1), (CZ, 1)):
+            masked = jnp.where(has[a], jnp.float32(weight), jnp.float32(0.0))
+            for h in range(0, CY, 8):
+
+                def put_layer(t, l, value):
+                    tau[t, z + 1, l, pl.ds(8 + h, 8), :] = value
+
+                stresses(load_cell(z, h), masked, (XZ, YZ, ZZ), put_layer)
+
+
+        @pl.when(jnp.logical_not(is_main))
+        def _():
+            for z in (0, 1, CZ - 2, CZ - 1):
+                advance_early(z, 0)
+            for copy in fringe[1:3]:
+                copy.start()
+
+        arrive(ROWS)
         for side in range(2):
             y = edge(side, 0)
             outward = -1 if side == 0 else 1
@@ -351,22 +414,6 @@
 
             stresses(load_edge, weight, range(6), put_edge, base_edge, finish_edge)
 
-        for j in (CORNER, CORNER + 1, CORNER + 2, CORNER + 3, Z_DOWN, Z_UP):
-            copy, _, receives = jobs[j]
-            guarded(receives, copy.wait_recv)
-        place_rows(k)
-        own_layer(0)
-        own_layer(CZ - 1)
-
-        for z, a in ((-1, -1), (CZ, 1)):
-            masked = jnp.where(has[a], jnp.float32(weight), jnp.float32(0.0))
-            for h in range(0, CY, 8):
-
-                def put_layer(t, l, value):
-                    tau[t, z + 1, l, pl.ds(8 + h, 8), :] = value
-
-                stresses(load_cell(z, h), masked, (XZ, YZ, ZZ), put_layer)
-
         for side in range(2):
             y = -1 if side == 0 else CY
             outward = -1 if side == 0 else 1
@@ -383,31 +430,30 @@
 
             stresses(load_row, weight, (XY, YY, YZ), put_row)
 
-        def advance(tiles, z, carry):
-            for h in range(0, CY, 8):
-
-                def at(t, l, dz=0, dy=0):
-                    return tau_layers[t * ZT + z + 1 + dz, pl.ds(l * PY + 8 + h + dy, 8), :]
-
-                for c, (ty, tz) in enumerate(((XY, XZ), (YY, YZ), (YZ, ZZ))):
-                    for l in tiles:
-                        value = acc[c, z, l, pl.ds(h, 8), :] + (at(ty, l, dy=1) - at(ty, l, dy=-1))
-                        value = value + (at(tz, l, dz=1) - at(tz, l, dz=-1))
-                        u[k + 1, c, z + 2, l, pl.ds(8 + h, 8), :] = value
+        def put_next(c, z, h, l, value):
+            u[k + 1, c, z + 2, l, pl.ds(8 + h, 8), :] = value
+
+        def advance_first(z, carry):
+            advance((0,), z, put_next)
             return carry
 
-        fringe = remote(k, BOX, u.at[k + 1, :, own_z, 0, inner], arrived.at[k], {"box": 1})
-        lax.fori_loop(0, CZ, functools.partial(advance, (0,)), 0)
+        def advance_rest(z, carry):
+            advance((1, 2, 3), z, put_next)
+            return carry
+
+        lax.fori_loop(0, CZ, advance_first, 0, unroll=4)
 
         @pl.when(jnp.logical_not(is_main))
         def _():
-            fringe.start()
-
-        lax.fori_loop(0, CZ, functools.partial(advance, (1, 2, 3)), 0)
+            for copy in fringe[3:]:
+                copy.start()
+
+        lax.fori_loop(0, CZ, advance_rest, 0, unroll=2)
 
         @pl.when(is_main)
         def _():
-            fringe.wait_recv()
+            for copy in fringe:
+                copy.wait_recv()
 
             def mix(z, carry):
                 for c in range(3):
@@ -418,7 +464,7 @@
                         )
                 return carry
 
-            lax.fori_loop(0, CZ, mix, 0)
+            lax.fori_loop(0, CZ, mix, 0, unroll=4)
 
         return jobs, fringe
 
@@ -429,21 +475,20 @@
     def rotate_out(z, carry):
         for c in range(3):
             for h in range(0, CY, 8):
-                tiles = [
-                    pltpu.roll(u[3, c, z + 2, (l - q) & (LT - 1), pl.ds(8 + h, 8), :], r, 1)
-                    for l in range(-1, LT)
-                ]
+                tiles = turned_tiles([u[3, c, z + 2, l, pl.ds(8 + h, 8), :] for l in range(LT)], -1)
+                tiles = [pltpu.roll(t, r, 1) for t in tiles]
                 for l in range(LT):
                     out[0, c, z, pl.ds(h, 8), pl.ds(l * LANES, LANES)] = jnp.where(
-                        turned_in, tiles[l + 1], tiles[l]
+                        turned_in, tiles[l], tiles[l - 1]
                     )
         return carry
 
-    lax.fori_loop(0, CZ, rotate_out, 0)
+    lax.fori_loop(0, CZ, rotate_out, 0, unroll=4)
     for jobs, fringe in sent:
         for copy, sends, _ in jobs:
             guarded(sends, copy.wait_send)
-        pl.when(jnp.logical_not(is_main))(fringe.wait_send)
+        for copy in fringe:
+            pl.when(jnp.logical_not(is_main))(copy.wait_send)
 
 
 def solution(mesh):
@@ -458,20 +503,19 @@
                 pl.BlockSpec(memory_space=pltpu.SMEM),
                 pl.BlockSpec(memory_space=pltpu.SMEM),
                 pl.BlockSpec(memory_space=pltpu.VMEM),
-                pl.BlockSpec(memory_space=pltpu.MemorySpace.HBM),
+                pl.BlockSpec(memory_space=pltpu.VMEM),
             ],
             out_specs=pl.BlockSpec(memory_space=pltpu.VMEM),
             scratch_shapes=[
                 pltpu.VMEM((4, 3, ZU, LT, PY, LANES), f32),
                 pltpu.VMEM((6, ZT, LT, PY, LANES), f32),
                 pltpu.VMEM((3, CZ, LT, CY, LANES), f32),
-                pltpu.VMEM((3, CZ, LT, CY, LANES), f32),
                 pltpu.VMEM((CZ, LT, CY, LANES), f32),
                 pltpu.VMEM((3, 2, 2, 3, LT, CZ + 16, LANES), f32),
                 pltpu.VMEM((2, LT, CZ, LANES), f32),
                 pltpu.VMEM((3, 2, 3, ZT, LT, 2, LANES), f32),
                 pltpu.VMEM((3, 3, CZ, CY, LANES), f32),
-                pltpu.SemaphoreType.DMA((LT,)),
+                pltpu.VMEM((3, 3, CZ, CY, LANES), f32),
                 pltpu.SemaphoreType.DMA((3, COPIES)),
                 pltpu.SemaphoreType.DMA((3, COPIES)),
             ],

time: 41.9 us -> 36.8 us (0.88)
  Pallas kernels: 38.4 us -> 33.1 us
    pallas_call x1, Pallas kernels: 38.4 us -> 33.1 us  [per_device(): pl.pallas_call(functools.partial(kernel, nz, ny), out_shape=jax.ShapeDtyp...]
where the time goes in v3:
time: 36.8 us; the launch traced here: 36.5 us
  Pallas kernels  33.1 us (90%)
  local copies, waits for them, and re-layouts  2.03 us (6%)
  between operations  1.33 us (4%)
    pallas_call x1, Pallas kernels, per_device(): pl.pallas_call(functools.partial(kernel, nz, ny), out_shape=jax.ShapeDtyp...  33.1 us
    unnamed x5, local copies, waits for them, and re-layouts  2.03 us

profile of v3, /device:TPU:17, one launch (start us, length us, event | category | flops | bytes accessed | tf_op | source)
XLA Modules:
  0.0 36.5 jit_solution(5197358741384477905)
XLA Ops:
  0.7 0.0 copy-start.1
  1.3 0.0 copy-done.1
  1.3 0.0 copy-start
  1.3 1.1 %copy-done = f32[1,3,8,16,512]{4,3,2,1,0:T(8,128)S(1)} copy-done((f32[1,3,8,16,512]{4,3,2,1,0:T(8,128)S(1)}, f32[1,3,8,16,512]{4,3,2,1,0:T(8,128)}, u32[]{:S(2)}) %copy-start) | copy-done | bytes 786456
  2.5 33.1 %shard_map.46 = f32[1,3,8,16,512]{4,3,2,1,0:T(8,128)S(1)} custom-call(s32[1]{0:T(128)S(6)} %copy.7.start, s32[1,1]{1,0:T(1,128)S(6)} %copy.6.count, s32[1,512]{1,0:T(1,128)S(1)} %bitcast.1, f32[1,3,8,16,512]{4,3,2,1,0:T(8,128)S(1)} %copy-done), custom_call_target="tpu_custom_call" | custom-call | tf_op jit(solution)/shard_map/pallas_call | solution.py:499
  35.6 0.9 %copy.8 = f32[1,3,8,16,512]{4,3,2,1,0:T(8,128)} copy(f32[1,3,8,16,512]{4,3,2,1,0:T(8,128)S(1)} %shard_map.46) | data formatting | bytes 1572864
Async XLA Ops:
  0.7 0.7 %copy-start.1 = (s32[1,1,512]{2,1,0:T(1,128)S(1)}, s32[1,1,512]{2,1,0:T(1,128)}, u32[]{:S(2)}) copy-start(s32[1,1,512]{2,1,0:T(1,128)} %param.5) | copy-start | bytes 6148
  1.3 1.1 %copy-start = (f32[1,3,8,16,512]{4,3,2,1,0:T(8,128)S(1)}, f32[1,3,8,16,512]{4,3,2,1,0:T(8,128)}, u32[]{:S(2)}) copy-start(f32[1,3,8,16,512]{4,3,2,1,0:T(8,128)} %vel.1) | copy-start | bytes 2359300

commit v4 on v3

--- a/solution.py
+++ b/solution.py
@@ -31,7 +31,7 @@
 
 
 def kernel(
-    nz, ny, start, count, cells, vel, out, u, tau, acc, cnt, own, slots_of, ry, early, arrived, send_sem, recv_sem
+    nz, ny, start, count, cells_in, vel, out, cells, u, tau, acc, raw, cnt, own, slots_of, ry, early, arrived, io_sem, send_sem, recv_sem
 ):
     gz, gy, box = lax.axis_index("gz"), lax.axis_index("gy"), lax.axis_index("box")
     up, down = lax.rem(gy + 1, ny), lax.rem(gy + ny - 1, ny)
@@ -40,6 +40,14 @@
     has = {-1: has_below, 1: has_above}
     beside = {-1: down, 1: up}
 
+    loads = [
+        pltpu.make_async_copy(src, dst, io_sem.at[i])
+        for i, (src, dst) in enumerate(
+            ((vel.at[0], raw), (cells_in, cells))
+        )
+    ]
+    for copy in loads:
+        copy.start()
     barrier = pltpu.get_barrier_semaphore()
 
     def greet(where):
@@ -67,6 +75,8 @@
     tau_flat = tau.reshape(6 * ZT * SPAN, LANES)
     tau_layers = tau.reshape(6 * ZT, SPAN, LANES)
 
+    for copy in loads:
+        copy.wait()
     s = start[0]
     q = lax.shift_right_logical(s, 7)
     r = s & (LANES - 1)
@@ -83,7 +93,7 @@
         for c in range(3):
             for h in range(0, CY, 8):
                 tiles = turned_tiles(
-                    [vel[0, c, z, pl.ds(h, 8), l * LANES : (l + 1) * LANES] for l in range(LT)], 1
+                    [raw[c, z, pl.ds(h, 8), l * LANES : (l + 1) * LANES] for l in range(LT)], 1
                 )
                 tiles = [pltpu.roll(t, left, 1) for t in tiles]
                 for l in range(LT):
@@ -499,30 +509,35 @@
         return pl.pallas_call(
             functools.partial(kernel, nz, ny),
             out_shape=jax.ShapeDtypeStruct(velocity.shape, f32),
-            in_specs=[
-                pl.BlockSpec(memory_space=pltpu.SMEM),
-                pl.BlockSpec(memory_space=pltpu.SMEM),
-                pl.BlockSpec(memory_space=pltpu.VMEM),
-                pl.BlockSpec(memory_space=pltpu.VMEM),
-            ],
+            in_specs=[pl.BlockSpec(memory_space=pltpu.SMEM)] * 2 + [pl.BlockSpec(memory_space=pltpu.MemorySpace.HBM)] * 2,
             out_specs=pl.BlockSpec(memory_space=pltpu.VMEM),
             scratch_shapes=[
+                pltpu.VMEM((1, turbine_cells.shape[-1]), jnp.int32),
                 pltpu.VMEM((4, 3, ZU, LT, PY, LANES), f32),
                 pltpu.VMEM((6, ZT, LT, PY, LANES), f32),
                 pltpu.VMEM((3, CZ, LT, CY, LANES), f32),
+                pltpu.VMEM((3, CZ, CY, NX), f32),
                 pltpu.VMEM((CZ, LT, CY, LANES), f32),
                 pltpu.VMEM((3, 2, 2, 3, LT, CZ + 16, LANES), f32),
                 pltpu.VMEM((2, LT, CZ, LANES), f32),
                 pltpu.VMEM((3, 2, 3, ZT, LT, 2, LANES), f32),
                 pltpu.VMEM((3, 3, CZ, CY, LANES), f32),
                 pltpu.VMEM((3, 3, CZ, CY, LANES), f32),
+                pltpu.SemaphoreType.DMA((2,)),
                 pltpu.SemaphoreType.DMA((3, COPIES)),
                 pltpu.SemaphoreType.DMA((3, COPIES)),
             ],
             compiler_params=pltpu.CompilerParams(
                 collective_id=0, has_side_effects=True, vmem_limit_bytes=48 << 20
             ),
-        )(fringe_start, turbine_count, turbine_cells.reshape(1, -1), velocity)
+        )(
+            fringe_start,
+            turbine_count,
+            *(
+                pltpu.with_memory_space_constraint(x, pltpu.MemorySpace.HBM)
+                for x in (turbine_cells.reshape(1, -1), velocity)
+            ),
+        )
 
     return jax.shard_map(
         per_device,

time: 36.8 us -> 35.7 us (0.970)
  local copies, waits for them, and re-layouts: 2.03 us -> 0.88 us
    unnamed x5 -> x1, local copies, waits for them, and re-layouts: 2.03 us -> 0.88 us
where the time goes in v4:
time: 35.7 us; the launch traced here: 35.4 us
  Pallas kernels  33.2 us (93%)
  between operations  1.3 us (4%)
  local copies, waits for them, and re-layouts  0.88 us (2%)
    pallas_call x1, Pallas kernels, per_device(): pl.pallas_call(functools.partial(kernel, nz, ny), out_shape=jax.ShapeDtyp...  33.2 us
    unnamed x1, local copies, waits for them, and re-layouts  0.88 us

profile of v4, /device:TPU:17, one launch (start us, length us, event | category | flops | bytes accessed | tf_op | source)
XLA Modules:
  0.0 35.4 jit_solution(13092820412750253933)
XLA Ops:
  1.3 33.2 %shard_map.46 = f32[1,3,8,16,512]{4,3,2,1,0:T(8,128)S(1)} custom-call(s32[1]{0:T(128)S(6)} %copy.7.start, s32[1,1]{1,0:T(1,128)S(6)} %copy.6.count, s32[1,512]{1,0:T(1,128)} %bitcast.1, f32[1,3,8,16,512]{4,3,2,1,0:T(8,128)} %vel.1), custom_call_target="tpu_custom_call" | custom-call | tf_op jit(solution)/shard_map/pallas_call | solution.py:509
  34.5 0.9 %copy.8 = f32[1,3,8,16,512]{4,3,2,1,0:T(8,128)} copy(f32[1,3,8,16,512]{4,3,2,1,0:T(8,128)S(1)} %shard_map.46) | data formatting | bytes 1572864
